TPU v7x, 512 devices: a whole 4x8x8 slice. The times are simulated.
512 devices in a mesh: gx: 32 (over x_lo, z, core), gy: 16 (over y, x_hi).
Axes of the slice: x: 4 (x_hi: 2, x_lo: 2; x = x_hi * 2 + x_lo), y: 8, z: 8, core: 2. Of those that a mesh axis runs over, the one named last changes fastest.
Arguments:
- u_field: float32 [1024, 4096], P('gx', 'gy'), may hold values from -6 to 6
- v_field: float32 [1024, 4096], P('gx', 'gy'), may hold values from -6 to 6
- w_first: bfloat16 [9, 64, 2], replicated, may hold values from -1.5 to 1.5
- b_first: float32 [64], replicated, may hold values from -3 to 3
- w_second: bfloat16 [9, 64, 64], replicated, may hold values from -0.25 to 0.25
- b_second: float32 [64], replicated, may hold values from -3 to 3
- w_third: bfloat16 [9, 16, 64], replicated, may hold values from -0.25 to 0.25
- b_third: float32 [16], replicated, may hold values from -3 to 3
Outputs:
- u_next: float32 [1024, 4096], P('gx', 'gy')
- v_next: float32 [1024, 4096], P('gx', 'gy')
All inputs are finite; a program needn't handle non-finite values.
Results may differ from a plain program's by a relative error of at most 0.0023.
Values sent between devices are 32-bit elements; how exact they have to be, the bound alone decides.
A program may use at most 64 MiB of HBM per device.

v0:
```python
import math

import jax
import jax.numpy as jnp
from jax import lax
from jax.sharding import PartitionSpec as P

step_ratio = 0.4
stencil_base = (-0.0625, 0.5625, 0.5625, -0.0625)
block_height = 8
highest = lax.Precision.HIGHEST


def padded_2(value, sides, width):
    for axis, dim in sides:
        peers, length = (lax.axis_size(axis), value.shape[dim])
        up = [(i, (i + 1) % peers) for i in range(peers)]
        down = [(j, i) for i, j in up]
        last = lax.slice_in_dim(value, length - width, length, axis=dim)
        first = lax.slice_in_dim(value, 0, width, axis=dim)
        before = lax.ppermute(last, axis, up)
        after = lax.ppermute(first, axis, down)
        value = jnp.concatenate([before, value, after], axis=dim)
    return value


def from_behind(block, axis, distance):
    devices = range(lax.axis_size(axis))
    route = [((i - distance) % len(devices), i) for i in devices]
    return lax.ppermute(block, axis, route)


def convolve(inputs, kernel, offsets, height, breadth):
    summed = None
    for tap_index in range(9):
        shift_down = tap_index // 3
        shift_right = tap_index % 3
        window = inputs[:, shift_down : shift_down + height, shift_right : shift_right + breadth]
        term = jnp.einsum(
            "oc,chw->ohw", kernel[tap_index], window, preferred_element_type=jnp.float32
        )
        summed = term if summed is None else summed + term
    return summed + offsets[:, None, None]


def predict(features, layers, top_row, left_col, height, breadth):
    w_first, b_first, w_second, b_second, w_third, b_third = layers
    inputs = lax.dynamic_slice(
        features, (0, top_row, left_col), (features.shape[0], height + 6, breadth + 6)
    )
    first = jax.nn.relu(convolve(inputs, w_first, b_first, height + 4, breadth + 4)).astype(
        jnp.bfloat16
    )
    second = jax.nn.relu(convolve(first, w_second, b_second, height + 2, breadth + 2)).astype(
        jnp.bfloat16
    )
    return convolve(second, w_third, b_third, height, breadth)


def coefficients(features, layers, margin, first_col, breadth):
    height = features.shape[1] - 2 * margin
    initial = jnp.zeros((layers[4].shape[1], height, breadth), jnp.float32)

    def advance(position, outputs):
        start_row = position * block_height
        piece = predict(
            features, layers, start_row + margin - 3, margin - 3 + first_col, block_height, breadth
        )
        return lax.dynamic_update_slice(outputs, piece, (0, start_row, 0))

    return lax.fori_loop(0, height // block_height, advance, initial)


def fluxes(padded, coeff, margin, anchor, height, breadth):

    def sample(shift_down, shift_right):
        top_row = margin + anchor + shift_down
        left_col = margin + anchor + shift_right
        return padded[:, top_row : top_row + height, left_col : left_col + breadth]

    weights = coeff.reshape(2, 2, 4, height, breadth)
    weights = (
        jnp.asarray(stencil_base, jnp.float32)[:, None, None]
        + weights
        - jnp.mean(weights, axis=2, keepdims=True)
    )
    centre = sample(0, 0)
    east = (
        weights[0, :, 0] * sample(-1, 0)
        + weights[0, :, 1] * centre
        + weights[0, :, 2] * sample(1, 0)
        + weights[0, :, 3] * sample(2, 0)
    )
    north = (
        weights[1, :, 0] * sample(0, -1)
        + weights[1, :, 1] * centre
        + weights[1, :, 2] * sample(0, 1)
        + weights[1, :, 3] * sample(0, 2)
    )
    carry_x = 0.5 * (centre[0] + sample(1, 0)[0])
    carry_y = 0.5 * (centre[1] + sample(0, 1)[1])
    return (carry_x * east, carry_y * north)


def dft_table(length, sign):
    counter = jnp.arange(length, dtype=jnp.int32)
    phases = counter[:, None] * counter[None, :] % length
    phases = phases.astype(jnp.float32) * (sign * 2.0 * math.pi / length)
    return (jnp.cos(phases), jnp.sin(phases))


def rotate(spectra, cosine, sine, form):

    def product(matrix, values):
        return jnp.einsum(form, matrix, values, precision=highest)

    if spectra.shape[0] == 1:
        return jnp.stack([product(cosine, spectra[0]), product(sine, spectra[0])])
    real_part = spectra[0]
    imag_part = spectra[1]
    return jnp.stack(
        [
            product(cosine, real_part) - product(sine, imag_part),
            product(cosine, imag_part) + product(sine, real_part),
        ]
    )


def twiddle(spectra, phases):
    cosine = jnp.cos(phases)
    sine = jnp.sin(phases)
    real_part = spectra[0]
    imag_part = spectra[1]
    return jnp.stack([real_part * cosine - imag_part * sine, real_part * sine + imag_part * cosine])


def row_section(spectra, sign):
    members = lax.axis_size("gx")
    own_index = lax.axis_index("gx")
    length = spectra.shape[2]
    sub_rows = length // members
    whole = members * length
    local_cos, local_sin = dft_table(length, sign)
    if sign > 0:
        spectra = rotate(spectra, local_cos, local_sin, "mp,fpy->fmy")

    def through(pieces):
        group_cos, group_sin = dft_table(members, sign)
        cell_rows = own_index * sub_rows + jnp.arange(sub_rows, dtype=jnp.int32)
        frequency = jnp.arange(members, dtype=jnp.int32)
        phases = (frequency[:, None] * cell_rows[None, :] % whole).astype(jnp.float32) * (
            sign * 2.0 * math.pi / whole
        )
        if sign < 0:
            return twiddle(
                rotate(pieces, group_cos, group_sin, "ka,fasy->fksy"), phases[:, :, None]
            )
        return rotate(twiddle(pieces, phases[:, :, None]), group_cos, group_sin, "ak,fksy->fasy")[
            :1
        ]

    shaped = spectra.reshape(spectra.shape[0], 2, 1, length, spectra.shape[3])
    arrived = lax.all_to_all(shaped, "gx", split_axis=3, concat_axis=2, tiled=True)
    turned = through(arrived)
    returned = lax.all_to_all(turned, "gx", split_axis=2, concat_axis=3, tiled=True)
    returned = returned.reshape(returned.shape[0], 2, returned.shape[3], returned.shape[4])
    if sign < 0:
        returned = rotate(returned, local_cos, local_sin, "pm,fmy->fpy")
    return returned


def column_local(pieces, sign, members):
    length = pieces.shape[4]
    whole = members * length
    group_cos, group_sin = dft_table(members, sign)
    local_cos, local_sin = dft_table(length, sign)
    frequency = jnp.arange(members, dtype=jnp.int32)
    column_ids = jnp.arange(length, dtype=jnp.int32)
    phases = (frequency[:, None] * column_ids[None, :] % whole).astype(jnp.float32) * (
        sign * 2.0 * math.pi / whole
    )
    phases = phases[:, None, :]
    if sign < 0:
        turned = twiddle(rotate(pieces, group_cos, group_sin, "kb,fbpj->fkpj"), phases)
        return rotate(turned, local_cos, local_sin, "qj,fkpj->fkpq")
    turned = twiddle(rotate(pieces, local_cos, local_sin, "jq,fkpq->fkpj"), phases)
    return rotate(turned, group_cos, group_sin, "bk,fkpj->fbpj")


def column_out(spectra, sign):
    members = lax.axis_size("gy")
    shaped = spectra.reshape(2, 2, 1, spectra.shape[2], spectra.shape[3])
    arrived = lax.all_to_all(shaped, "gy", split_axis=3, concat_axis=2, tiled=True)
    return column_local(arrived, sign, members)


def column_home(spectra):
    returned = lax.all_to_all(spectra, "gy", split_axis=2, concat_axis=3, tiled=True)
    return returned.reshape(2, 2, returned.shape[3], returned.shape[4])


def wavenumber(counter, whole):
    signed = jnp.where(counter >= whole // 2, counter - whole, counter)
    return signed.astype(jnp.float32) * (2.0 * math.pi / whole)


def project(spectra, wave_x, wave_y):
    denominator = wave_x * wave_x + wave_y * wave_y
    denominator = jnp.where(denominator > 0, denominator, 1.0)
    shared = (wave_x * spectra[:, 0] + wave_y * spectra[:, 1]) / denominator
    return jnp.stack([spectra[:, 0] - wave_x * shared, spectra[:, 1] - wave_y * shared], axis=1)


def on_device(u_field, v_field, w_first, b_first, w_second, b_second, w_third, b_third):
    field = jnp.stack([u_field, v_field])
    height, breadth = u_field.shape
    layers = (w_first, b_first, w_second, b_second, w_third, b_third)
    padded = padded_2(field, (("gx", 1), ("gy", 2)), 3)
    features = padded.astype(jnp.bfloat16)
    coeff = coefficients(features, layers, 3, 0, breadth)
    east_now, north_now = fluxes(padded, coeff, 3, 0, height, breadth)
    below = from_behind(east_now[:, -1:, :], "gx", 1)
    beside = from_behind(north_now[:, :, -1:], "gy", 1)
    east_before = jnp.concatenate([below, east_now[:, :-1]], axis=1)
    north_before = jnp.concatenate([beside, north_now[:, :, :-1]], axis=2)
    star = field - step_ratio * (east_now - east_before + north_now - north_before)
    grid_x = height * lax.axis_size("gx")
    grid_y = breadth * lax.axis_size("gy")
    index_x = lax.axis_index("gx")
    index_y = lax.axis_index("gy")
    spectra = row_section(star[None], -1)
    spectra = column_home(column_out(spectra, -1))
    wave_x = wavenumber(
        index_x + lax.axis_size("gx") * jnp.arange(height, dtype=jnp.int32), grid_x
    )[:, None]
    wave_y = wavenumber(
        index_y + lax.axis_size("gy") * jnp.arange(breadth, dtype=jnp.int32), grid_y
    )[None, :]
    spectra = project(spectra, wave_x, wave_y)
    spectra = column_home(column_out(spectra, 1))
    result = row_section(spectra, 1)
    scale = 1.0 / (grid_x * grid_y)
    return (result[0, 0] * scale, result[0, 1] * scale)


def solution(mesh):
    return jax.shard_map(
        on_device,
        mesh=mesh,
        in_specs=(P("gx", "gy"), P("gx", "gy"), P(), P(), P(), P(), P(), P()),
        out_specs=(P("gx", "gy"), P("gx", "gy")),
        check_vma=False,
    )
```

profile of v0, /device:TPU:1, one launch (start us, length us, event | category | flops | bytes accessed | tf_op | source)
XLA Modules:
  0.0 219.3 jit_solution(6147832409521107079)
XLA Ops:
  0.7 0.8 fusion.226
  1.5 8.7 %collective-permute-start = (f32[2,3,256]{2,1,0:T(4,128)S(1)}, f32[2,3,256]{2,1,0:T(4,128)S(1)}, u32[]{:S(2)}, u32[]{:S(2)}) collective-permute-start(f32[2,3,256]{2,1,0:T(4,128)S(1)} %get-tuple-element.373), channel_id=1, source_target_pairs={{16,0},{32,16},{48,32},{64,48},{80,64},{96,80},{112,96},{128,112},... | collective-permute-start | bytes 18440 | tf_op jit(solution)/shard_map/ppermute | solution.py:22
  10.3 1.9 collective-permute-start.1
  12.2 4.7 %collective-permute-done.1 = f32[2,3,256]{2,1,0:T(4,128)S(1)} collective-permute-done((f32[2,3,256]{2,1,0:T(4,128)S(1)}, f32[2,3,256]{2,1,0:T(4,128)S(1)}, u32[]{:S(2)}, u32[]{:S(2)}) %collective-permute-start.1) | collective-permute-done | bytes 6176 | tf_op jit(solution)/shard_map/ppermute | solution.py:21
  17.8 7.3 %collective-permute-start.3 = (f32[2,38,3]{2,1,0:T(8,128)S(1)}, f32[2,38,3]{2,1,0:T(8,128)S(1)}, u32[]{:S(2)}, u32[]{:S(2)}) collective-permute-start(f32[2,38,3]{2,1,0:T(8,128)S(1)} %get-tuple-element.369), channel_id=1, source_target_pairs={{1,0},{2,1},{3,2},{4,3},{5,4},{6,5},{7,6},{8,7},{9,8},{10,9},{11,1... | collective-permute-start | bytes 2744 | tf_op jit(solution)/shard_map/ppermute | solution.py:22
  25.0 1.9 collective-permute-start.2
  29.3 4.1 %collective-permute-done.2 = f32[2,38,3]{2,1,0:T(8,128)S(1)} collective-permute-done((f32[2,38,3]{2,1,0:T(8,128)S(1)}, f32[2,38,3]{2,1,0:T(8,128)S(1)}, u32[]{:S(2)}, u32[]{:S(2)}) %collective-permute-start.2) | collective-permute-done | bytes 944 | tf_op jit(solution)/shard_map/ppermute | solution.py:21
  33.7 34.7 %while.17 = (s32[]{:T(128)}, f32[16,32,256]{2,1,0:T(8,128)S(1)}, bf16[2,38,262]{2,0,1:T(2,128)(2,1)S(1)}, bf16[9,64,2]{1,2,0:T(2,128)(2,1)S(1)}, f32[64]{0:T(128...) while((s32[]{:T(128)}, f32[16,32,256]{2,1,0:T(8,128)S(1)}, ...), condition=%wide.region_1.2_spmd, body=%wide.region_0.1_spmd.sunk | while | flops 239463184 | bytes 39334732 | solution.py:71
  69.2 1.9 collective-permute-start.4
  71.4 1.9 collective-permute-start.5
  73.4 6.3 %collective-permute-done.5 = f32[2,32,1]{2,1,0:T(8,128)S(1)} collective-permute-done((f32[2,32,1]{2,1,0:T(8,128)S(1)}, f32[2,32,1]{2,1,0:T(8,128)S(1)}, u32[]{:S(2)}, u32[]{:S(2)}) %collective-permute-start.5) | collective-permute-done | bytes 288 | tf_op jit(solution)/shard_map/ppermute | solution.py:30
  80.5 11.2 %all-to-all-start = ((f32[1,2,1,32,256]{4,1,2,0,3:T(2,128)}), f32[1,2,1,32,256]{4,1,2,0,3:T(2,128)S(1)}, u32[]{:S(2)}, u32[]{:S(2)}) async-start(f32[1,2,1,32,256]{4,1,2,0,3:T(2,128)} %copy.117), calls=%async_computation | async-start | bytes 131072 | tf_op jit(solution)/shard_map/all_to_all | solution.py:163
  91.7 8.0 %all-to-all-done = f32[1,2,1,32,256]{4,1,2,0,3:T(2,128)S(1)} async-done(((f32[1,2,1,32,256]{4,1,2,0,3:T(2,128)}), f32[1,2,1,32,256]{4,1,2,0,3:T(2,128)S(1)}, u32[]{:S(2)}, u32[]{:S(2)}) %all-to-all-start) | async-done | bytes 65568 | tf_op jit(solution)/shard_map/all_to_all | solution.py:163
  100.4 12.9 %all_to_all.32 = f32[2,2,32,1,256]{4,1,3,0,2:T(2,128)S(1)} all-to-all(f32[2,2,32,1,256]{4,1,3,0,2:T(2,128)S(1)} %copy.119), channel_id=1, replica_groups=mesh['gx'=32,'gy'=16] {'gx'}, dimensions={2} | all-to-all | bytes 262144 | tf_op jit(solution)/shard_map/all_to_all | solution.py:165
  115.2 3.9 %all-to-all-start.2 = ((f32[2,2,1,32,256]{4,1,0,2,3:T(2,128)}), f32[2,2,1,32,256]{4,1,0,2,3:T(2,128)S(1)}, u32[]{:S(2)}, u32[]{:S(2)}) async-start(f32[2,2,1,32,256]{4,1,0,2,3:T(2,128)} %copy.122), calls=%async_computation.2 | async-start | bytes 262144 | tf_op jit(solution)/shard_map/all_to_all | solution.py:193
  119.3 9.9 %all-to-all-done.2 = f32[2,2,1,32,256]{4,1,0,2,3:T(2,128)S(1)} async-done(((f32[2,2,1,32,256]{4,1,0,2,3:T(2,128)}), f32[2,2,1,32,256]{4,1,0,2,3:T(2,128)S(1)}, u32[]{:S(2)}, u32[]{:S(2)}) %all-to-all-start.2) | async-done | bytes 131104 | tf_op jit(solution)/shard_map/all_to_all | solution.py:193
  130.2 1.3 fusion.126
  131.5 1.3 fusion.124
  132.9 1.3 fusion.113
  134.2 1.3 fusion.112
  136.3 3.5 %all-to-all-start.3 = ((f32[2,2,16,2,256]{4,3,1,0,2:T(2,128)}), f32[2,2,16,2,256]{4,3,1,0,2:T(2,128)S(1)}, u32[]{:S(2)}, u32[]{:S(2)}) async-start(f32[2,2,16,2,256]{4,3,1,0,2:T(2,128)} %copy.127), calls=%async_computation.3 | async-start | bytes 262144 | tf_op jit(solution)/shard_map/all_to_all | solution.py:198
  139.9 10.0 %all-to-all-done.3 = f32[2,2,16,2,256]{4,3,1,0,2:T(2,128)S(1)} async-done(((f32[2,2,16,2,256]{4,3,1,0,2:T(2,128)}), f32[2,2,16,2,256]{4,3,1,0,2:T(2,128)S(1)}, u32[]{:S(2)}, u32[]{:S(2)}) %all-to-all-start.3) | async-done | bytes 131104 | tf_op jit(solution)/shard_map/all_to_all | solution.py:198
  151.0 3.7 %all-to-all-start.4 = ((f32[2,2,1,32,256]{4,1,0,2,3:T(2,128)}), f32[2,2,1,32,256]{4,1,0,2,3:T(2,128)S(1)}, u32[]{:S(2)}, u32[]{:S(2)}) async-start(f32[2,2,1,32,256]{4,1,0,2,3:T(2,128)} %copy.131), calls=%async_computation.4 | async-start | bytes 262144 | tf_op jit(solution)/shard_map/all_to_all | solution.py:193
  154.8 9.8 %all-to-all-done.4 = f32[2,2,1,32,256]{4,1,0,2,3:T(2,128)S(1)} async-done(((f32[2,2,1,32,256]{4,1,0,2,3:T(2,128)}), f32[2,2,1,32,256]{4,1,0,2,3:T(2,128)S(1)}, u32[]{:S(2)}, u32[]{:S(2)}) %all-to-all-start.4) | async-done | bytes 131104 | tf_op jit(solution)/shard_map/all_to_all | solution.py:193
  164.6 1.3 fusion.120
  165.9 1.3 fusion.118
  167.2 1.3 convolution_subtract_fusion.5
  168.5 1.3 convolution_add_fusion.28
  171.1 12.7 %all_to_all.33 = f32[2,2,16,2,256]{4,3,1,0,2:T(2,128)S(1)} all-to-all(f32[2,2,16,2,256]{4,3,1,0,2:T(2,128)S(1)} %copy.136), channel_id=1, replica_groups=mesh['gx'=32,'gy'=16] {'gy'}, dimensions={2} | all-to-all | bytes 262144 | tf_op jit(solution)/shard_map/all_to_all | solution.py:198
  185.7 10.1 %all-to-all-start.6 = ((f32[2,2,1,32,256]{4,1,0,2,3:T(2,128)}), f32[2,2,1,32,256]{4,1,0,2,3:T(2,128)S(1)}, u32[]{:S(2)}, u32[]{:S(2)}) async-start(f32[2,2,1,32,256]{4,1,0,2,3:T(2,128)} %copy.143), calls=%async_computation.6 | async-start | bytes 262144 | tf_op jit(solution)/shard_map/all_to_all | solution.py:163
  195.8 9.0 %all-to-all-done.6 = f32[2,2,1,32,256]{4,1,0,2,3:T(2,128)S(1)} async-done(((f32[2,2,1,32,256]{4,1,0,2,3:T(2,128)}), f32[2,2,1,32,256]{4,1,0,2,3:T(2,128)S(1)}, u32[]{:S(2)}, u32[]{:S(2)}) %all-to-all-start.6) | async-done | bytes 131104 | tf_op jit(solution)/shard_map/all_to_all | solution.py:163
  205.5 12.5 %all_to_all.34 = f32[1,2,32,1,256]{4,1,3,0,2:T(2,128)S(1)} all-to-all(f32[1,2,32,1,256]{4,1,3,0,2:T(2,128)S(1)} %copy.146), channel_id=1, replica_groups=mesh['gx'=32,'gy'=16] {'gx'}, dimensions={2} | all-to-all | bytes 131072 | tf_op jit(solution)/shard_map/all_to_all | solution.py:165
  (207 shorter events, 49.9 us)
Async XLA Ops:
  0.6 33.0 %copy-start.4 = (bf16[9,64,2]{1,2,0:T(2,128)(2,1)S(1)}, bf16[9,64,2]{1,2,0:T(2,128)(2,1)}, u32[]{:S(2)}) copy-start(bf16[9,64,2]{1,2,0:T(2,128)(2,1)} %param.13) | copy-start | bytes 6916
  0.6 33.0 %copy-start.5 = (f32[64]{0:T(128)S(1)}, f32[64]{0:T(128)}, u32[]{:S(2)}) copy-start(f32[64]{0:T(128)} %param.14) | copy-start | bytes 772
  0.7 33.0 %copy-start = (bf16[9,64,64]{2,1,0:T(8,128)(2,1)S(1)}, bf16[9,64,64]{2,1,0:T(8,128)(2,1)}, u32[]{:S(2)}) copy-start(bf16[9,64,64]{2,1,0:T(8,128)(2,1)} %param.15) | copy-start | bytes 221188
  0.7 33.0 %copy-start.6 = (f32[64]{0:T(128)S(1)}, f32[64]{0:T(128)}, u32[]{:S(2)}) copy-start(f32[64]{0:T(128)} %param.16) | copy-start | bytes 772
  0.7 33.0 %copy-start.3 = (bf16[9,16,64]{2,1,0:T(8,128)(2,1)S(1)}, bf16[9,16,64]{2,1,0:T(8,128)(2,1)}, u32[]{:S(2)}) copy-start(bf16[9,16,64]{2,1,0:T(8,128)(2,1)} %param.17) | copy-start | bytes 55300
  0.7 33.0 %copy-start.7 = (f32[16]{0:T(128)S(1)}, f32[16]{0:T(128)}, u32[]{:S(2)}) copy-start(f32[16]{0:T(128)} %param.18) | copy-start | bytes 196
  1.5 10.7 %collective-permute-start = (f32[2,3,256]{2,1,0:T(4,128)S(1)}, f32[2,3,256]{2,1,0:T(4,128)S(1)}, u32[]{:S(2)}, u32[]{:S(2)}) collective-permute-start(f32[2,3,256]{2,1,0:T(4,128)S(1)} %get-tuple-element.373), channel_id=1, source_target_pairs={{16,0},{32,16},{48,32},{64,48},{80,64},{96,80},{112,96},{128,112},... | collective-permute-start | bytes 18440 | tf_op jit(solution)/shard_map/ppermute | solution.py:22
  10.3 6.6 %collective-permute-start.1 = (f32[2,3,256]{2,1,0:T(4,128)S(1)}, f32[2,3,256]{2,1,0:T(4,128)S(1)}, u32[]{:S(2)}, u32[]{:S(2)}) collective-permute-start(f32[2,3,256]{2,1,0:T(4,128)S(1)} %get-tuple-element.372), channel_id=1, source_target_pairs={{0,16},{16,32},{32,48},{48,64},{64,80},{80,96},{96,112},{112,128},... | collective-permute-start | bytes 18440 | tf_op jit(solution)/shard_map/ppermute | solution.py:21
  17.8 11.5 %collective-permute-start.3 = (f32[2,38,3]{2,1,0:T(8,128)S(1)}, f32[2,38,3]{2,1,0:T(8,128)S(1)}, u32[]{:S(2)}, u32[]{:S(2)}) collective-permute-start(f32[2,38,3]{2,1,0:T(8,128)S(1)} %get-tuple-element.369), channel_id=1, source_target_pairs={{1,0},{2,1},{3,2},{4,3},{5,4},{6,5},{7,6},{8,7},{9,8},{10,9},{11,1... | collective-permute-start | bytes 2744 | tf_op jit(solution)/shard_map/ppermute | solution.py:22
  25.0 8.4 %collective-permute-start.2 = (f32[2,38,3]{2,1,0:T(8,128)S(1)}, f32[2,38,3]{2,1,0:T(8,128)S(1)}, u32[]{:S(2)}, u32[]{:S(2)}) collective-permute-start(f32[2,38,3]{2,1,0:T(8,128)S(1)} %get-tuple-element.368), channel_id=1, source_target_pairs={{0,1},{1,2},{2,3},{3,4},{4,5},{5,6},{6,7},{7,8},{8,9},{9,10},{10,1... | collective-permute-start | bytes 2744 | tf_op jit(solution)/shard_map/ppermute | solution.py:21
  33.7 34.8 %copy-start.8 = (f32[4]{0:T(128)S(1)}, f32[4]{0:T(128)}, u32[]{:S(2)}) copy-start(f32[4]{0:T(128)} %constant.251.clone) | copy-start | bytes 52
  68.3 0.8 copy-start.1
  68.4 0.8 copy-start.2
  69.2 10.5 %collective-permute-start.4 = (f32[2,1,256]{2,1,0:T(1,128)S(1)}, f32[2,1,256]{2,1,0:T(1,128)S(1)}, u32[]{:S(2)}, u32[]{:S(2)}) collective-permute-start(f32[2,1,256]{2,1,0:T(1,128)S(1)} %slice.912), channel_id=1, source_target_pairs={{496,0},{0,16},{16,32},{32,48},{48,64},{64,80},{80,96},{96,112},{1... | collective-permute-start | bytes 6152 | tf_op jit(solution)/shard_map/ppermute | solution.py:30
  71.4 8.3 %collective-permute-start.5 = (f32[2,32,1]{2,1,0:T(8,128)S(1)}, f32[2,32,1]{2,1,0:T(8,128)S(1)}, u32[]{:S(2)}, u32[]{:S(2)}) collective-permute-start(f32[2,32,1]{2,1,0:T(8,128)S(1)} %slice.920), channel_id=1, source_target_pairs={{15,0},{0,1},{1,2},{2,3},{3,4},{4,5},{5,6},{6,7},{7,8},{8,9},{9,10... | collective-permute-start | bytes 776 | tf_op jit(solution)/shard_map/ppermute | solution.py:30
  80.5 19.3 %all-to-all-start = ((f32[1,2,1,32,256]{4,1,2,0,3:T(2,128)}), f32[1,2,1,32,256]{4,1,2,0,3:T(2,128)S(1)}, u32[]{:S(2)}, u32[]{:S(2)}) async-start(f32[1,2,1,32,256]{4,1,2,0,3:T(2,128)} %copy.117), calls=%async_computation | async-start | bytes 131072 | tf_op jit(solution)/shard_map/all_to_all | solution.py:163
  115.2 14.0 %all-to-all-start.2 = ((f32[2,2,1,32,256]{4,1,0,2,3:T(2,128)}), f32[2,2,1,32,256]{4,1,0,2,3:T(2,128)S(1)}, u32[]{:S(2)}, u32[]{:S(2)}) async-start(f32[2,2,1,32,256]{4,1,0,2,3:T(2,128)} %copy.122), calls=%async_computation.2 | async-start | bytes 262144 | tf_op jit(solution)/shard_map/all_to_all | solution.py:193
  136.3 13.6 %all-to-all-start.3 = ((f32[2,2,16,2,256]{4,3,1,0,2:T(2,128)}), f32[2,2,16,2,256]{4,3,1,0,2:T(2,128)S(1)}, u32[]{:S(2)}, u32[]{:S(2)}) async-start(f32[2,2,16,2,256]{4,3,1,0,2:T(2,128)} %copy.127), calls=%async_computation.3 | async-start | bytes 262144 | tf_op jit(solution)/shard_map/all_to_all | solution.py:198
  151.0 13.6 %all-to-all-start.4 = ((f32[2,2,1,32,256]{4,1,0,2,3:T(2,128)}), f32[2,2,1,32,256]{4,1,0,2,3:T(2,128)S(1)}, u32[]{:S(2)}, u32[]{:S(2)}) async-start(f32[2,2,1,32,256]{4,1,0,2,3:T(2,128)} %copy.131), calls=%async_computation.4 | async-start | bytes 262144 | tf_op jit(solution)/shard_map/all_to_all | solution.py:193
  185.7 19.1 %all-to-all-start.6 = ((f32[2,2,1,32,256]{4,1,0,2,3:T(2,128)}), f32[2,2,1,32,256]{4,1,0,2,3:T(2,128)S(1)}, u32[]{:S(2)}, u32[]{:S(2)}) async-start(f32[2,2,1,32,256]{4,1,0,2,3:T(2,128)} %copy.143), calls=%async_computation.6 | async-start | bytes 262144 | tf_op jit(solution)/shard_map/all_to_all | solution.py:163
where the time goes:
time: 220 us; the launch traced here: 219 us
  waiting for transfers between devices  61.9 us (28%)
  starting transfers between devices  56.1 us (26%)
  matrix products  49.4 us (22%)
  blocking collectives  38.1 us (17%)
  local copies, waits for them, and re-layouts  6.66 us (3%)
  other arithmetic  5.2 us (2%)
    dot_general x108, matrix products, convolve(): jnp.einsum('oc,chw->ohw', kernel[tap_index], window, preferred_element_ty...  33.6 us
    all_to_all x2, blocking collectives, row_section(): lax.all_to_all(turned, 'gx', split_axis=2, concat_axis=3, tiled=True)  25.4 us
    all_to_all x2, starting transfers between devices, row_section(): lax.all_to_all(shaped, 'gx', split_axis=3, concat_axis=2, tiled=True)  21.2 us
    all_to_all x2, waiting for transfers between devices, column_out(): lax.all_to_all(shaped, 'gy', split_axis=3, concat_axis=2, tiled=True)  19.7 us
    all_to_all x2, waiting for transfers between devices, row_section(): lax.all_to_all(shaped, 'gx', split_axis=3, concat_axis=2, tiled=True)  17.1 us
    ppermute x2, starting transfers between devices, padded_2(): after = lax.ppermute(first, axis, down)  16 us
    dot_general x28, matrix products, product(): return jnp.einsum(form, matrix, values, precision=highest)  15.8 us
    all_to_all x1, blocking collectives, column_home(): lax.all_to_all(spectra, 'gy', split_axis=2, concat_axis=3, tiled=True)  12.7 us
  transfers between devices with their start and end apart: 11, of which 8 were waited for; matrix products, arithmetic and copies ran while one was open for 1% of the time, Pallas kernels for 0%

commit v1 on v0

v1 whole, which is shorter than its diff:
```python
import functools
import math

import jax
import jax.numpy as jnp
import ml_dtypes
import numpy as np
from jax import lax
from jax.experimental import pallas as pl
from jax.experimental.pallas import tpu as pltpu
from jax.sharding import PartitionSpec as P

step_ratio = 0.4
stencil_base = (-0.0625, 0.5625, 0.5625, -0.0625)
block_height = 8
GX = 32
GY = 16
NX = 1024
NY = 4096
f32 = jnp.float32
bf16 = jnp.bfloat16


def padded_2(value, sides, width):
    for axis, dim in sides:
        peers, length = (lax.axis_size(axis), value.shape[dim])
        up = [(i, (i + 1) % peers) for i in range(peers)]
        down = [(j, i) for i, j in up]
        last = lax.slice_in_dim(value, length - width, length, axis=dim)
        first = lax.slice_in_dim(value, 0, width, axis=dim)
        before = lax.ppermute(last, axis, up)
        after = lax.ppermute(first, axis, down)
        value = jnp.concatenate([before, value, after], axis=dim)
    return value


def from_behind(block, axis, distance):
    devices = range(lax.axis_size(axis))
    route = [((i - distance) % len(devices), i) for i in devices]
    return lax.ppermute(block, axis, route)


def convolve(inputs, kernel, offsets, height, breadth):
    summed = None
    for tap_index in range(9):
        shift_down = tap_index // 3
        shift_right = tap_index % 3
        window = inputs[:, shift_down : shift_down + height, shift_right : shift_right + breadth]
        term = jnp.einsum(
            "oc,chw->ohw", kernel[tap_index], window, preferred_element_type=jnp.float32
        )
        summed = term if summed is None else summed + term
    return summed + offsets[:, None, None]


def predict(features, layers, top_row, left_col, height, breadth):
    w_first, b_first, w_second, b_second, w_third, b_third = layers
    inputs = lax.dynamic_slice(
        features, (0, top_row, left_col), (features.shape[0], height + 6, breadth + 6)
    )
    first = jax.nn.relu(convolve(inputs, w_first, b_first, height + 4, breadth + 4)).astype(
        jnp.bfloat16
    )
    second = jax.nn.relu(convolve(first, w_second, b_second, height + 2, breadth + 2)).astype(
        jnp.bfloat16
    )
    return convolve(second, w_third, b_third, height, breadth)


def coefficients(features, layers, margin, first_col, breadth):
    height = features.shape[1] - 2 * margin
    initial = jnp.zeros((layers[4].shape[1], height, breadth), jnp.float32)

    def advance(position, outputs):
        start_row = position * block_height
        piece = predict(
            features, layers, start_row + margin - 3, margin - 3 + first_col, block_height, breadth
        )
        return lax.dynamic_update_slice(outputs, piece, (0, start_row, 0))

    return lax.fori_loop(0, height // block_height, advance, initial)


def fluxes(padded, coeff, margin, anchor, height, breadth):

    def sample(shift_down, shift_right):
        top_row = margin + anchor + shift_down
        left_col = margin + anchor + shift_right
        return padded[:, top_row : top_row + height, left_col : left_col + breadth]

    weights = coeff.reshape(2, 2, 4, height, breadth)
    weights = (
        jnp.asarray(stencil_base, jnp.float32)[:, None, None]
        + weights
        - jnp.mean(weights, axis=2, keepdims=True)
    )
    centre = sample(0, 0)
    east = (
        weights[0, :, 0] * sample(-1, 0)
        + weights[0, :, 1] * centre
        + weights[0, :, 2] * sample(1, 0)
        + weights[0, :, 3] * sample(2, 0)
    )
    north = (
        weights[1, :, 0] * sample(0, -1)
        + weights[1, :, 1] * centre
        + weights[1, :, 2] * sample(0, 1)
        + weights[1, :, 3] * sample(0, 2)
    )
    carry_x = 0.5 * (centre[0] + sample(1, 0)[0])
    carry_y = 0.5 * (centre[1] + sample(0, 1)[1])
    return (carry_x * east, carry_y * north)


def star_fields(u_field, v_field, layers):
    field = jnp.stack([u_field, v_field])
    height, breadth = u_field.shape
    padded = padded_2(field, (("gx", 1), ("gy", 2)), 3)
    features = padded.astype(jnp.bfloat16)
    coeff = coefficients(features, layers, 3, 0, breadth)
    east_now, north_now = fluxes(padded, coeff, 3, 0, height, breadth)
    below = from_behind(east_now[:, -1:, :], "gx", 1)
    beside = from_behind(north_now[:, :, -1:], "gy", 1)
    east_before = jnp.concatenate([below, east_now[:, :-1]], axis=1)
    north_before = jnp.concatenate([beside, north_now[:, :, :-1]], axis=2)
    return field - step_ratio * (east_now - east_before + north_now - north_before)


def split_bf16(table):
    hi = table.astype(np.float32).astype(ml_dtypes.bfloat16)
    lo = (table - hi.astype(np.float64)).astype(np.float32).astype(ml_dtypes.bfloat16)
    return hi, lo


def real_left(matrix):
    return np.block([[matrix.real, -matrix.imag], [matrix.imag, matrix.real]])


def triple_left(table):
    hi, lo = split_bf16(table)
    return np.concatenate([hi, hi, lo], axis=1)


def root(product, whole):
    return np.exp(-2j * np.pi * (product % whole) / whole)


@functools.cache
def tables():
    n16, n32, n256 = np.arange(16), np.arange(32), np.arange(256)
    paired = np.concatenate([2 * n16, 2 * n16 + 1])
    dft16 = real_left(root(np.outer(n16, n16), 16))
    conj_in = np.concatenate([np.ones(16), -np.ones(16)])
    t_a = triple_left(dft16 * conj_in[None, :])
    t_a2 = triple_left(dft16 * conj_in[:, None])
    mid = root(np.outer(n256, n256), 256)
    t_b = np.stack(split_bf16(np.block([[mid.real, mid.imag], [-mid.imag, mid.real]])))
    tw = root(np.outer(n16, n256), 4096)
    tw = np.stack([tw.real, tw.imag]).astype(np.float32)
    t_r = triple_left(real_left(root(np.outer(paired, n32), 32)))
    t_r2 = triple_left(real_left(root(np.outer(n32, paired), 32)))
    t_p = triple_left(real_left(root(np.outer(n32, paired), 32)))
    t_p2 = triple_left(real_left(root(np.outer(paired, n32), 32)))
    t_s = np.stack([t_r, t_r2, t_p, t_p2])
    twr = np.zeros((16, 32, 4), np.float32)
    for r in range(2):
        row = root(np.outer(2 * n16 + r, paired), 1024)
        twr[:, :, 2 * r] = row.real
        twr[:, :, 2 * r + 1] = row.imag
    return np.stack([t_a, t_a2]), t_b, tw, t_s, twr


def triple(value):
    hi = value.astype(bf16)
    lo = (value - hi.astype(f32)).astype(bf16)
    return jnp.concatenate([hi, lo, hi], axis=0)


def left_product(table, value):
    return jnp.dot(table, triple(value), preferred_element_type=f32)


def right_product(value, t_b):
    rows = value.shape[0]
    hi = value.astype(bf16)
    lo = (value - hi.astype(f32)).astype(bf16)
    both = jnp.dot(jnp.concatenate([hi, lo], axis=0), t_b[0], preferred_element_type=f32)
    return both[:rows] + both[rows:] + jnp.dot(hi, t_b[1], preferred_element_type=f32)


def spectral_kernel(star, t_a, t_b, tw, t_s, twr, out, st, s1, r1, s2, r2, s3, r3, s4, r4, s5, r5, s6, r6, ssem, rsem):
    a = lax.axis_index("gx")
    b = lax.axis_index("gy")
    MESH = pl.DeviceIdType.MESH

    barrier = pltpu.get_barrier_semaphore()

    def greet_x(d, _):
        pl.semaphore_signal(barrier, inc=1, device_id={"gx": (a + d) % GX}, device_id_type=MESH)
        return 0

    def greet_y(d, _):
        pl.semaphore_signal(barrier, inc=1, device_id={"gy": (b + d) % GY}, device_id_type=MESH)
        return 0

    lax.fori_loop(1, GX, greet_x, 0)
    lax.fori_loop(1, GY, greet_y, 0)
    pl.semaphore_wait(barrier, GX + GY - 2)

    def far_first(step, size):
        half = (step + 1) // 2
        return size // 2 + half - 2 * half * (step % 2)

    def send_y(stage, src, dst):
        def go(step, _):
            peer = (b + far_first(step, GY)) % GY
            pltpu.make_async_remote_copy(
                src.at[peer], dst.at[b], ssem.at[stage], rsem.at[stage],
                device_id={"gy": peer}, device_id_type=MESH,
            ).start()
            return 0

        lax.fori_loop(0, GY - 1, go, 0)
        dst[b] = src[b]

    def send_x(stage, src_of, dst_of):
        def go(step, _):
            peer = (a + far_first(step, GX)) % GX
            pltpu.make_async_remote_copy(
                src_of(peer), dst_of(a), ssem.at[stage], rsem.at[stage],
                device_id={"gx": peer}, device_id_type=MESH,
            ).start()
            return 0

        lax.fori_loop(0, GX - 1, go, 0)

    def wait_for(sem, like):
        pltpu.make_async_copy(like, like, sem).wait()

    for c in range(2):
        for h in range(2):
            st[c * 2 + h] = star[c, :, h * 128 : h * 128 + 128]
    for c in range(2):
        for r in range(2):
            for h in range(2):
                s1[:, c * 4 + r * 2 + h, :] = st[c * 2 + h, pl.ds(r, 16, stride=2), :]
    send_y(0, s1, r1)

    shape = (32, 256)
    m2 = lax.broadcasted_iota(jnp.int32, shape, 0)
    lane = lax.broadcasted_iota(jnp.int32, shape, 1)
    kx = 2 * b + lane // 128 + 32 * m2
    ky = a // 2 + 16 * ((a % 2) * 128 + lane % 128)
    wx = jnp.where(kx >= NX // 2, kx - NX, kx).astype(f32) * (2.0 * math.pi / NX)
    wy = jnp.where(ky >= NY // 2, ky - NY, ky).astype(f32) * (2.0 * math.pi / NY)
    den = wx * wx + wy * wy
    origin = (kx == 0) & (ky == 0)
    den = jnp.where(origin, 1.0, den)
    scale = 1.0 / (NX * NY)
    share = scale / den
    g_re = 0.5 * (wy * wy - wx * wx) * share
    g_im = -(wx * wy) * share
    g_im = jnp.where((kx == NX // 2) != (ky == NY // 2), 0.0, g_im)
    g_one = jnp.where(origin, 0.5 * scale, g_re)
    g_two = jnp.where(origin, -0.5 * scale, g_re)

    wait_for(rsem.at[0], r1.at[pl.ds(0, GY - 1)])

    tr, ti = tw[0], tw[1]
    x = jnp.concatenate(
        [
            jnp.concatenate([r1[:, c * 4 + k, :] for k in range(4)], axis=1)
            for c in range(2)
        ],
        axis=0,
    )
    y = left_product(t_a[0], x)
    lines = []
    for r in range(2):
        yr, yi = y[:16, r * 256 : r * 256 + 256], y[16:, r * 256 : r * 256 + 256]
        lines.append(jnp.concatenate([yr * tr - yi * ti, yr * ti + yi * tr], axis=1))
    o = right_product(jnp.concatenate(lines, axis=0), t_b)
    for c in range(2):
        for r in range(2):
            for h in range(2):
                at = c * 256 + h * 128
                s2[:, h, c * 2 + r, :] = o[r * 16 : r * 16 + 16, at : at + 128]
    send_x(1, lambda peer: s2.at[peer // 2, peer % 2], lambda me: r2.at[me])
    r2[a] = s2[a // 2, a % 2]
    wait_for(rsem.at[1], r2.at[pl.ds(0, GX - 1)])

    x = jnp.concatenate(
        [jnp.concatenate([r2[:, c * 2 + r, :] for r in range(2)], axis=1) for c in range(2)], axis=0
    )
    y = left_product(t_s[0], x)
    column = twr[b]
    for r in range(2):
        cr, ci = column[:, 2 * r : 2 * r + 1], column[:, 2 * r + 1 : 2 * r + 2]
        yr, yi = y[:32, r * 128 : r * 128 + 128], y[32:, r * 128 : r * 128 + 128]
        for c, value in enumerate((yr * cr - yi * ci, yr * ci + yi * cr)):
            for t in range(2):
                s3[:, c * 4 + r * 2 + t, :] = value[t * 16 : t * 16 + 16]
    send_y(2, s3, r3)
    wait_for(rsem.at[2], r3.at[pl.ds(0, GY - 1)])
    x = jnp.concatenate(
        [
            jnp.concatenate([r3[:, c * 4 + r * 2 + t, :] for t in range(2)], axis=1)
            for c in range(2)
            for r in range(2)
        ],
        axis=0,
    )
    y = left_product(t_s[2], x)
    yr, yi = y[:32], y[32:]

    q = jnp.concatenate([g_one * yr - g_im * yi, -(g_two * yi + g_im * yr)], axis=0)

    y = left_product(t_s[3], q)
    for c in range(2):
        for r in range(2):
            for t in range(2):
                row = c * 32 + r * 16
                s4[:, c * 4 + r * 2 + t, :] = y[row : row + 16, t * 128 : t * 128 + 128]
    send_y(3, s4, r4)
    wait_for(rsem.at[3], r4.at[pl.ds(0, GY - 1)])
    halves = [[], []]
    for r in range(2):
        cr, ci = column[:, 2 * r : 2 * r + 1], column[:, 2 * r + 1 : 2 * r + 2]
        yr, yi = (
            jnp.concatenate([r4[:, c * 4 + r * 2 + t, :] for t in range(2)], axis=0) for c in range(2)
        )
        halves[0].append(yr * cr - yi * ci)
        halves[1].append(yr * ci + yi * cr)
    x = jnp.concatenate([jnp.concatenate(half, axis=1) for half in halves], axis=0)
    y = left_product(t_s[1], x)
    for c in range(2):
        for r in range(2):
            s5[:, c * 2 + r, :] = y[c * 32 : c * 32 + 32, r * 128 : r * 128 + 128]
    send_x(4, lambda peer: s5.at[peer], lambda me: r5.at[me // 2, me % 2])
    r5[a // 2, a % 2] = s5[a]
    wait_for(rsem.at[4], s5.at[pl.ds(0, GX - 1)])
    x = jnp.concatenate(
        [
            jnp.concatenate([r5[:, h, c * 2 + r, :] for c in range(2) for h in range(2)], axis=1)
            for r in range(2)
        ],
        axis=0,
    )
    o = right_product(x, t_b)
    lines = [[], []]
    for r in range(2):
        yr, yi = o[r * 16 : r * 16 + 16, :256], o[r * 16 : r * 16 + 16, 256:]
        lines[0].append(yr * tr - yi * ti)
        lines[1].append(yr * ti + yi * tr)
    x = jnp.concatenate([jnp.concatenate(line, axis=1) for line in lines], axis=0)
    y = left_product(t_a[1], x)
    for c in range(2):
        for k in range(4):
            s6[:, c * 4 + k, :] = y[c * 16 : c * 16 + 16, k * 128 : k * 128 + 128]
    send_y(5, s6, r6)
    wait_for(rsem.at[5], r6.at[pl.ds(0, GY - 1)])
    for c in range(2):
        for r in range(2):
            for h in range(2):
                st[c * 2 + h, pl.ds(r, 16, stride=2), :] = r6[:, c * 4 + r * 2 + h, :]
    for c in range(2):
        for h in range(2):
            lanes = slice(h * 128, h * 128 + 128)
            out[c, :, lanes] = 0.5 * star[c, :, lanes] + st[c * 2 + h]

    for stage, buffer in ((0, s1), (2, s3), (3, s4), (5, s6)):
        wait_for(ssem.at[stage], buffer.at[pl.ds(0, GY - 1)])
    wait_for(ssem.at[1], r2.at[pl.ds(0, GX - 1)])
    wait_for(ssem.at[4], s5.at[pl.ds(0, GX - 1)])


def project(star):
    whole = pl.BlockSpec(memory_space=pltpu.VMEM)
    y_buf = pltpu.VMEM((16, 8, 128), f32)
    x_buf = pltpu.VMEM((32, 4, 128), f32)
    pair_buf = pltpu.VMEM((16, 2, 4, 128), f32)
    t_a, t_b, tw, t_s, twr = (jnp.asarray(t) for t in tables())
    return pl.pallas_call(
        spectral_kernel,
        out_shape=jax.ShapeDtypeStruct((2, 32, 256), f32),
        in_specs=[whole] * 6,
        out_specs=whole,
        scratch_shapes=[
            pltpu.VMEM((4, 32, 128), f32),
            y_buf, y_buf, pair_buf, x_buf, y_buf, y_buf, y_buf, y_buf, x_buf, pair_buf, y_buf, y_buf,
            pltpu.SemaphoreType.DMA((6,)),
            pltpu.SemaphoreType.DMA((6,)),
        ],
        compiler_params=pltpu.CompilerParams(collective_id=0, has_side_effects=True),
        name="spectral",
    )(star, t_a, t_b, tw, t_s, twr)


def on_device(u_field, v_field, w_first, b_first, w_second, b_second, w_third, b_third):
    layers = (w_first, b_first, w_second, b_second, w_third, b_third)
    star = star_fields(u_field, v_field, layers)
    result = project(star)
    return result[0], result[1]


def solution(mesh):
    return jax.shard_map(
        on_device,
        mesh=mesh,
        in_specs=(P("gx", "gy"), P("gx", "gy"), P(), P(), P(), P(), P(), P()),
        out_specs=(P("gx", "gy"), P("gx", "gy")),
        check_vma=False,
    )
```

time: 220 us -> 131 us (0.60)
  Pallas kernels: 0 us -> 48.2 us
  waiting for transfers between devices: 61.9 us -> 15.1 us
  blocking collectives: 38.1 us -> 0 us
  starting transfers between devices: 56.1 us -> 23.7 us
  matrix products: 49.4 us -> 33.7 us
  local copies, waits for them, and re-layouts: 6.66 us -> 2.54 us
    pallas_call x0 -> x1, Pallas kernels: none -> 48.2 us  [project(): pl.pallas_call(spectral_kernel, out_shape=jax.ShapeDtypeStruct((2, 32, 25...]
    all_to_all x5 -> x0, waiting for transfers between devices: 46.7 us -> none  [the longest x2 19.7 us: column_out(): lax.all_to_all(shaped, 'gy', split_axis=3, concat_axis=2, tiled=True)]
    all_to_all x3 -> x0, blocking collectives: 38.1 us -> none  [the longest x2 25.4 us: row_section(): lax.all_to_all(turned, 'gx', split_axis=2, concat_axis=3, tiled=True)]
    all_to_all x5 -> x0, starting transfers between devices: 32.4 us -> none  [the longest x2 21.2 us: row_section(): lax.all_to_all(shaped, 'gx', split_axis=3, concat_axis=2, tiled=True)]
    dot_general x28 -> x0, matrix products: 15.8 us -> none  [product(): return jnp.einsum(form, matrix, values, precision=highest)]
    reshape x3 -> x0, local copies, waits for them, and re-layouts: 2.27 us -> none  [the longest x2 1.51 us: column_out(): shaped = spectra.reshape(2, 2, 1, spectra.shape[2], spectra.shape[3])]
  transfers between devices with their start and end apart: 11 -> 6, of which waited for: 8 -> 3; matrix products, arithmetic and copies ran while one was open for 1% -> 2% of each run, Pallas kernels for 0% -> 0%
where the time goes in v1:
time: 131 us; the launch traced here: 130 us
  Pallas kernels  48.2 us (37%)
  matrix products  33.7 us (26%)
  starting transfers between devices  23.7 us (18%)
  waiting for transfers between devices  15.1 us (12%)
  other arithmetic  5.24 us (4%)
  local copies, waits for them, and re-layouts  2.54 us (2%)
    pallas_call x1, Pallas kernels, project(): pl.pallas_call(spectral_kernel, out_shape=jax.ShapeDtypeStruct((2, 32, 25...  48.2 us
    dot_general x108, matrix products, convolve(): jnp.einsum('oc,chw->ohw', kernel[tap_index], window, preferred_element_ty...  33.7 us
    ppermute x2, starting transfers between devices, padded_2(): after = lax.ppermute(first, axis, down)  16 us
    ppermute x2, waiting for transfers between devices, padded_2(): before = lax.ppermute(last, axis, up)  8.75 us
    ppermute x2, waiting for transfers between devices, from_behind(): return lax.ppermute(block, axis, route)  6.35 us
    ppermute x2, starting transfers between devices, padded_2(): before = lax.ppermute(last, axis, up)  3.84 us
    ppermute x2, starting transfers between devices, from_behind(): return lax.ppermute(block, axis, route)  3.83 us
  transfers between devices with their start and end apart: 6, of which 3 were waited for; matrix products, arithmetic and copies ran while one was open for 2% of the time, Pallas kernels for 0%

profile of v1, /device:TPU:1, one launch (start us, length us, event | category | flops | bytes accessed | tf_op | source)
XLA Modules:
  0.0 130.2 jit_solution(5289645039981557013)
XLA Ops:
  0.7 0.8 fusion.125
  1.5 8.7 %collective-permute-start = (f32[2,3,256]{2,1,0:T(4,128)S(1)}, f32[2,3,256]{2,1,0:T(4,128)S(1)}, u32[]{:S(2)}, u32[]{:S(2)}) collective-permute-start(f32[2,3,256]{2,1,0:T(4,128)S(1)} %get-tuple-element.330), channel_id=1, source_target_pairs={{16,0},{32,16},{48,32},{64,48},{80,64},{96,80},{112,96},{128,112},... | collective-permute-start | bytes 18440 | tf_op jit(solution)/shard_map/ppermute | solution.py:32
  10.3 1.9 %collective-permute-start.1 = (f32[2,3,256]{2,1,0:T(4,128)S(1)}, f32[2,3,256]{2,1,0:T(4,128)S(1)}, u32[]{:S(2)}, u32[]{:S(2)}) collective-permute-start(f32[2,3,256]{2,1,0:T(4,128)S(1)} %get-tuple-element.329), channel_id=1, source_target_pairs={{0,16},{16,32},{32,48},{48,64},{64,80},{80,96},{96,112},{112,128},... | collective-permute-start | bytes 18440 | tf_op jit(solution)/shard_map/ppermute | solution.py:31
  12.2 4.7 %collective-permute-done.1 = f32[2,3,256]{2,1,0:T(4,128)S(1)} collective-permute-done((f32[2,3,256]{2,1,0:T(4,128)S(1)}, f32[2,3,256]{2,1,0:T(4,128)S(1)}, u32[]{:S(2)}, u32[]{:S(2)}) %collective-permute-start.1) | collective-permute-done | bytes 6176 | tf_op jit(solution)/shard_map/ppermute | solution.py:31
  16.9 0.8 pad_maximum_fusion.3
  17.8 7.3 %collective-permute-start.3 = (f32[2,38,3]{2,1,0:T(8,128)S(1)}, f32[2,38,3]{2,1,0:T(8,128)S(1)}, u32[]{:S(2)}, u32[]{:S(2)}) collective-permute-start(f32[2,38,3]{2,1,0:T(8,128)S(1)} %get-tuple-element.326), channel_id=1, source_target_pairs={{1,0},{2,1},{3,2},{4,3},{5,4},{6,5},{7,6},{8,7},{9,8},{10,9},{11,1... | collective-permute-start | bytes 2744 | tf_op jit(solution)/shard_map/ppermute | solution.py:32
  25.0 1.9 %collective-permute-start.2 = (f32[2,38,3]{2,1,0:T(8,128)S(1)}, f32[2,38,3]{2,1,0:T(8,128)S(1)}, u32[]{:S(2)}, u32[]{:S(2)}) collective-permute-start(f32[2,38,3]{2,1,0:T(8,128)S(1)} %get-tuple-element.325), channel_id=1, source_target_pairs={{0,1},{1,2},{2,3},{3,4},{4,5},{5,6},{6,7},{7,8},{8,9},{9,10},{10,1... | collective-permute-start | bytes 2744 | tf_op jit(solution)/shard_map/ppermute | solution.py:31
  27.0 0.8 pad_maximum_fusion.2
  27.8 0.8 fusion.123
  28.5 0.8 fusion.126
  29.3 4.1 %collective-permute-done.2 = f32[2,38,3]{2,1,0:T(8,128)S(1)} collective-permute-done((f32[2,38,3]{2,1,0:T(8,128)S(1)}, f32[2,38,3]{2,1,0:T(8,128)S(1)}, u32[]{:S(2)}, u32[]{:S(2)}) %collective-permute-start.2) | collective-permute-done | bytes 944 | tf_op jit(solution)/shard_map/ppermute | solution.py:31
  33.7 34.8 %while.17 = (s32[]{:T(128)}, f32[16,32,256]{2,1,0:T(8,128)S(1)}, bf16[2,38,262]{2,0,1:T(2,128)(2,1)S(1)}, bf16[9,64,2]{1,2,0:T(2,128)(2,1)S(1)}, f32[64]{0:T(128...) while((s32[]{:T(128)}, f32[16,32,256]{2,1,0:T(8,128)S(1)}, ...), condition=%wide.region_1.2_spmd, body=%wide.region_0.1_spmd.sunk | while | flops 239463184 | bytes 39334732 | solution.py:81
  34.4 0.4 convolution_add_fusion.46
  35.6 0.4 convolution_add_fusion.49
  36.3 0.4 convolution_add_fusion.51
  36.7 0.4 fusion.243
  39.9 0.4 fusion.245
  43.1 0.4 convolution_add_fusion.46
  44.3 0.4 convolution_add_fusion.49
  45.4 0.4 fusion.243
  48.6 0.4 fusion.245
  54.1 0.4 fusion.243
  57.2 0.4 fusion.245
  62.8 0.4 fusion.243
  65.9 0.4 fusion.245
  68.7 0.5 copy-done.1
  69.3 1.9 %collective-permute-start.4 = (f32[2,1,256]{2,1,0:T(1,128)S(1)}, f32[2,1,256]{2,1,0:T(1,128)S(1)}, u32[]{:S(2)}, u32[]{:S(2)}) collective-permute-start(f32[2,1,256]{2,1,0:T(1,128)S(1)} %slice.847), channel_id=1, source_target_pairs={{496,0},{0,16},{16,32},{32,48},{48,64},{64,80},{80,96},{96,112},{1... | collective-permute-start | bytes 6152 | tf_op jit(solution)/shard_map/ppermute | solution.py:40
  71.5 1.9 %collective-permute-start.5 = (f32[2,32,1]{2,1,0:T(8,128)S(1)}, f32[2,32,1]{2,1,0:T(8,128)S(1)}, u32[]{:S(2)}, u32[]{:S(2)}) collective-permute-start(f32[2,32,1]{2,1,0:T(8,128)S(1)} %slice.855), channel_id=1, source_target_pairs={{15,0},{0,1},{1,2},{2,3},{3,4},{4,5},{5,6},{6,7},{7,8},{8,9},{9,10... | collective-permute-start | bytes 776 | tf_op jit(solution)/shard_map/ppermute | solution.py:40
  73.5 6.3 %collective-permute-done.5 = f32[2,32,1]{2,1,0:T(8,128)S(1)} collective-permute-done((f32[2,32,1]{2,1,0:T(8,128)S(1)}, f32[2,32,1]{2,1,0:T(8,128)S(1)}, u32[]{:S(2)}, u32[]{:S(2)}) %collective-permute-start.5) | collective-permute-done | bytes 288 | tf_op jit(solution)/shard_map/ppermute | solution.py:40
  79.8 0.7 fusion.119.star
  80.5 48.2 %spectral.1 = f32[2,32,256]{2,1,0:T(8,128)} custom-call(f32[2,32,256]{2,1,0:T(8,128)} %fusion.119.star, bf16[2,32,96]{2,1,0:T(8,128)(2,1)} %constant.123.clone.t_a, bf16[2,512,512]{2,1,0:T(8,128)(2,1)} %constant.124.clone.t_b, f32[2,16,256]{2,1,0:T(8,128)} %constant.125.clone.tw, bf16[4,64,192]{2,1,0:T(8,128)(2,1)} %constant.126.clone.t_s, ...), custom_call_target="tpu_custom_call" | custom-call | tf_op jit(solution)/shard_map/spectral/pallas_call | solution.py:383
  128.8 1.4 %slice_bitcast_fusion.9 = (f32[32,256]{1,0:T(8,128)}, f32[32,256]{1,0:T(8,128)}) fusion(f32[2,32,256]{2,1,0:T(8,128)} %spectral.1), kind=kLoop, calls=%fused_computation.181 | loop fusion | bytes 131072 | tf_op jit(solution)/shard_map/squeeze | solution.py:403
  (134 shorter events, 29.8 us)
Async XLA Ops:
  0.6 33.0 %copy-start.4 = (bf16[9,64,2]{1,2,0:T(2,128)(2,1)S(1)}, bf16[9,64,2]{1,2,0:T(2,128)(2,1)}, u32[]{:S(2)}) copy-start(bf16[9,64,2]{1,2,0:T(2,128)(2,1)} %param.18) | copy-start | bytes 6916
  0.6 33.0 %copy-start.5 = (f32[64]{0:T(128)S(1)}, f32[64]{0:T(128)}, u32[]{:S(2)}) copy-start(f32[64]{0:T(128)} %param.19) | copy-start | bytes 772
  0.7 33.0 %copy-start = (bf16[9,64,64]{2,1,0:T(8,128)(2,1)S(1)}, bf16[9,64,64]{2,1,0:T(8,128)(2,1)}, u32[]{:S(2)}) copy-start(bf16[9,64,64]{2,1,0:T(8,128)(2,1)} %param.20) | copy-start | bytes 221188
  0.7 33.0 %copy-start.6 = (f32[64]{0:T(128)S(1)}, f32[64]{0:T(128)}, u32[]{:S(2)}) copy-start(f32[64]{0:T(128)} %param.21) | copy-start | bytes 772
  0.7 33.0 %copy-start.3 = (bf16[9,16,64]{2,1,0:T(8,128)(2,1)S(1)}, bf16[9,16,64]{2,1,0:T(8,128)(2,1)}, u32[]{:S(2)}) copy-start(bf16[9,16,64]{2,1,0:T(8,128)(2,1)} %param.22) | copy-start | bytes 55300
  0.7 33.0 %copy-start.7 = (f32[16]{0:T(128)S(1)}, f32[16]{0:T(128)}, u32[]{:S(2)}) copy-start(f32[16]{0:T(128)} %param.23) | copy-start | bytes 196
  1.5 10.7 %collective-permute-start = (f32[2,3,256]{2,1,0:T(4,128)S(1)}, f32[2,3,256]{2,1,0:T(4,128)S(1)}, u32[]{:S(2)}, u32[]{:S(2)}) collective-permute-start(f32[2,3,256]{2,1,0:T(4,128)S(1)} %get-tuple-element.330), channel_id=1, source_target_pairs={{16,0},{32,16},{48,32},{64,48},{80,64},{96,80},{112,96},{128,112},... | collective-permute-start | bytes 18440 | tf_op jit(solution)/shard_map/ppermute | solution.py:32
  10.3 6.6 %collective-permute-start.1 = (f32[2,3,256]{2,1,0:T(4,128)S(1)}, f32[2,3,256]{2,1,0:T(4,128)S(1)}, u32[]{:S(2)}, u32[]{:S(2)}) collective-permute-start(f32[2,3,256]{2,1,0:T(4,128)S(1)} %get-tuple-element.329), channel_id=1, source_target_pairs={{0,16},{16,32},{32,48},{48,64},{64,80},{80,96},{96,112},{112,128},... | collective-permute-start | bytes 18440 | tf_op jit(solution)/shard_map/ppermute | solution.py:31
  17.8 11.5 %collective-permute-start.3 = (f32[2,38,3]{2,1,0:T(8,128)S(1)}, f32[2,38,3]{2,1,0:T(8,128)S(1)}, u32[]{:S(2)}, u32[]{:S(2)}) collective-permute-start(f32[2,38,3]{2,1,0:T(8,128)S(1)} %get-tuple-element.326), channel_id=1, source_target_pairs={{1,0},{2,1},{3,2},{4,3},{5,4},{6,5},{7,6},{8,7},{9,8},{10,9},{11,1... | collective-permute-start | bytes 2744 | tf_op jit(solution)/shard_map/ppermute | solution.py:32
  25.0 8.4 %collective-permute-start.2 = (f32[2,38,3]{2,1,0:T(8,128)S(1)}, f32[2,38,3]{2,1,0:T(8,128)S(1)}, u32[]{:S(2)}, u32[]{:S(2)}) collective-permute-start(f32[2,38,3]{2,1,0:T(8,128)S(1)} %get-tuple-element.325), channel_id=1, source_target_pairs={{0,1},{1,2},{2,3},{3,4},{4,5},{5,6},{6,7},{7,8},{8,9},{9,10},{10,1... | collective-permute-start | bytes 2744 | tf_op jit(solution)/shard_map/ppermute | solution.py:31
  33.7 34.9 %copy-start.8 = (f32[4]{0:T(128)S(1)}, f32[4]{0:T(128)}, u32[]{:S(2)}) copy-start(f32[4]{0:T(128)} %constant.122.clone) | copy-start | bytes 52
  68.5 0.8 copy-start.1
  68.5 0.8 copy-start.2
  69.3 10.5 %collective-permute-start.4 = (f32[2,1,256]{2,1,0:T(1,128)S(1)}, f32[2,1,256]{2,1,0:T(1,128)S(1)}, u32[]{:S(2)}, u32[]{:S(2)}) collective-permute-start(f32[2,1,256]{2,1,0:T(1,128)S(1)} %slice.847), channel_id=1, source_target_pairs={{496,0},{0,16},{16,32},{32,48},{48,64},{64,80},{80,96},{96,112},{1... | collective-permute-start | bytes 6152 | tf_op jit(solution)/shard_map/ppermute | solution.py:40
  71.5 8.3 %collective-permute-start.5 = (f32[2,32,1]{2,1,0:T(8,128)S(1)}, f32[2,32,1]{2,1,0:T(8,128)S(1)}, u32[]{:S(2)}, u32[]{:S(2)}) collective-permute-start(f32[2,32,1]{2,1,0:T(8,128)S(1)} %slice.855), channel_id=1, source_target_pairs={{15,0},{0,1},{1,2},{2,3},{3,4},{4,5},{5,6},{6,7},{7,8},{8,9},{9,10... | collective-permute-start | bytes 776 | tf_op jit(solution)/shard_map/ppermute | solution.py:40

commit v2 on v1

--- a/solution.py
+++ b/solution.py
@@ -12,7 +12,6 @@
 
 step_ratio = 0.4
 stencil_base = (-0.0625, 0.5625, 0.5625, -0.0625)
-block_height = 8
 GX = 32
 GY = 16
 NX = 1024
@@ -21,109 +20,221 @@
 bf16 = jnp.bfloat16
 
 
-def padded_2(value, sides, width):
-    for axis, dim in sides:
-        peers, length = (lax.axis_size(axis), value.shape[dim])
-        up = [(i, (i + 1) % peers) for i in range(peers)]
-        down = [(j, i) for i, j in up]
-        last = lax.slice_in_dim(value, length - width, length, axis=dim)
-        first = lax.slice_in_dim(value, 0, width, axis=dim)
-        before = lax.ppermute(last, axis, up)
-        after = lax.ppermute(first, axis, down)
-        value = jnp.concatenate([before, value, after], axis=dim)
-    return value
-
-
-def from_behind(block, axis, distance):
-    devices = range(lax.axis_size(axis))
-    route = [((i - distance) % len(devices), i) for i in devices]
-    return lax.ppermute(block, axis, route)
-
-
-def convolve(inputs, kernel, offsets, height, breadth):
-    summed = None
-    for tap_index in range(9):
-        shift_down = tap_index // 3
-        shift_right = tap_index % 3
-        window = inputs[:, shift_down : shift_down + height, shift_right : shift_right + breadth]
-        term = jnp.einsum(
-            "oc,chw->ohw", kernel[tap_index], window, preferred_element_type=jnp.float32
+PITCH = 272
+SHIFTS = (4, 3, 2, 1, 0, -1)
+
+
+def nt(left, right):
+    return lax.dot_general(left, right, (((1,), (1,)), ((), ())), preferred_element_type=f32)
+
+
+def front_kernel(
+    u, v, w1, b1, w2, b2, w3, b3, out,
+    rows_in, cols_in, corner_in, fs, k1, k2, k3, x1, x2, cf, fx, ssem, rsem,
+):
+    a = lax.axis_index("gx")
+    b = lax.axis_index("gy")
+    MESH = pl.DeviceIdType.MESH
+    moves = [(dx, dy) for dx in (-1, 0, 1) for dy in (-1, 0, 1) if (dx, dy) != (0, 0)]
+
+    def at(dx, dy):
+        return {"gx": (a + dx + GX) % GX, "gy": (b + dy + GY) % GY}
+
+    barrier = pltpu.get_barrier_semaphore()
+    for dx, dy in moves:
+        pl.semaphore_signal(barrier, inc=1, device_id=at(dx, dy), device_id_type=MESH)
+    pl.semaphore_wait(barrier, len(moves))
+
+    copies = []
+    for n, (dx, dy) in enumerate(moves):
+        rows = {-1: slice(0, 8), 0: slice(0, 32), 1: slice(24, 32)}[dx]
+        cols = {-1: slice(0, 128), 0: slice(0, 256), 1: slice(128, 256)}[dy]
+        for c, field in enumerate((u, v)):
+            if dx and dy:
+                dst = corner_in.at[(dx + 1) // 2, (dy + 1) // 2, c]
+            elif dx:
+                dst = rows_in.at[(dx + 1) // 2, c]
+            else:
+                dst = cols_in.at[(dy + 1) // 2, c]
+            copy = pltpu.make_async_remote_copy(
+                field.at[rows, cols], dst, ssem.at[2 * n + c], rsem.at[2 * n + c],
+                device_id=at(dx, dy), device_id_type=MESH,
+            )
+            copy.start()
+            copies.append(copy)
+
+    k1[...] = jnp.zeros_like(k1)
+    k2[...] = jnp.zeros_like(k2)
+    k3[...] = jnp.zeros_like(k3)
+    for dj in range(3):
+        for dr in range(3):
+            tap = 3 * dr + dj
+            for o in range(4):
+                x = o + dr
+                for c in range(2):
+                    k1[(dj * 2 + c) * 8 + x : (dj * 2 + c) * 8 + x + 1, o * 64 : o * 64 + 64] = w1[
+                        tap, c : c + 1, :
+                    ].astype(f32)
+                k2[dj, o * 64 : o * 64 + 64, x * 64 : x * 64 + 64] = w2[tap]
+                k3[dj * 64 + o * 16 : dj * 64 + o * 16 + 16, x * 64 : x * 64 + 64] = w3[tap]
+    bias1 = jnp.concatenate([b1[...]] * 4, axis=1)
+    bias2 = jnp.concatenate([b2[...]] * 4, axis=1)
+    x1[:, pl.ds(10 * PITCH, 16), :] = jnp.zeros((2, 16, 128), f32)
+    x2[pl.ds(9 * PITCH, 384), :] = jnp.zeros((384, 256), bf16)
+
+    for copy in copies:
+        copy.wait()
+
+    lane = lax.broadcasted_iota(jnp.int32, (8, 128), 1)
+    for c, field in enumerate((u, v)):
+        for g in range(6):
+            if g in (0, 5):
+                e = 1 if g == 0 else 0
+                tiles = [
+                    corner_in[e, 1, c], rows_in[e, c, :, 0:128], rows_in[e, c, :, 128:256], corner_in[e, 0, c],
+                ]
+            else:
+                rows = slice(g * 8 - 8, g * 8)
+                tiles = [
+                    cols_in[1, c, rows, :], field[rows, 0:128], field[rows, 128:256], cols_in[0, c, rows, :],
+                ]
+            for n, s in enumerate(SHIFTS):
+                if s == 0:
+                    for k in range(3):
+                        fs[n, c, k, g * 8 : g * 8 + 8, :] = tiles[k + 1]
+                    continue
+                turned = [pltpu.roll(tile, s % 128, 1) for tile in tiles]
+                for k in range(3):
+                    if s > 0:
+                        value = jnp.where(lane < s, turned[k], turned[k + 1])
+                    elif k < 2:
+                        value = jnp.where(lane >= 128 + s, turned[k + 2], turned[k + 1])
+                    else:
+                        value = turned[k + 1]
+                    fs[n, c, k, g * 8 : g * 8 + 8, :] = value
+
+    def layer_1(i, _):
+        patch = jnp.concatenate(
+            [
+                jnp.concatenate([fs[dj, c, k, pl.ds(4 * i + 4, 8), :] for k in range(3)], axis=1)
+                for dj in range(3)
+                for c in range(2)
+            ],
+            axis=0,
+        ).astype(bf16)
+        y = lax.dot_general(
+            patch, k1[...].astype(bf16), (((0,), (0,)), ((), ())), preferred_element_type=f32
         )
-        summed = term if summed is None else summed + term
-    return summed + offsets[:, None, None]
-
-
-def predict(features, layers, top_row, left_col, height, breadth):
+        y = jnp.maximum(y[:PITCH] + bias1, 0.0)
+        start = pl.multiple_of(i * PITCH, 8)
+        x1[0, pl.ds(start, PITCH), :] = y[:, :128]
+        x1[1, pl.ds(start, PITCH), :] = y[:, 128:]
+        return 0
+
+    lax.fori_loop(0, 10, layer_1, 0)
+
+    CHUNK = 3 * PITCH
+
+    def layer_2(i, _):
+        start = i * CHUNK
+
+        def piece(half, offset):
+            return x1[half, pl.ds(start + offset, CHUNK), :].astype(bf16)
+
+        y = None
+        for dj in range(3):
+            left = jnp.concatenate([piece(0, dj), piece(1, dj)], axis=1)
+            term = nt(left, k2[dj, :, 0:256])
+            y = term if y is None else y + term
+        left = jnp.concatenate([piece(0, PITCH), piece(0, PITCH + 1)], axis=1)
+        y = y + nt(left, jnp.concatenate([k2[0, :, 256:384], k2[1, :, 256:384]], axis=1))
+        y = y + nt(piece(0, PITCH + 2), k2[2, :, 256:384])
+        y = jnp.maximum(y + bias2, 0.0).astype(bf16)
+        x2[pl.ds(pl.multiple_of(start, 16), CHUNK), :] = y
+        return 0
+
+    lax.fori_loop(0, 3, layer_2, 0)
+
+    def layer_3(i, _):
+        start = pl.multiple_of(i * PITCH, 16)
+        after = pl.multiple_of((i + 1) * PITCH, 16)
+        y = nt(k3[:, 0:256], x2[pl.ds(start, 384), :]) + nt(k3[:, 256:384], x2[pl.ds(after, 384), 0:128])
+        y = y[0:64] + pltpu.roll(y[64:128], 383, 1) + pltpu.roll(y[128:192], 382, 1)
+        for o in range(4):
+            for k in range(3):
+                cf[k, pl.ds(4 * i + o, 16, stride=40), :] = y[o * 16 : o * 16 + 16, k * 128 : k * 128 + 128]
+        return 0
+
+    lax.fori_loop(0, 9, layer_3, 0)
+
+    def field_at(c, s, down, k, count=40):
+        return fs[SHIFTS.index(s), c, k, pl.ds(7 + down, count), :]
+
+    stepped = [[None] * 3 for _ in range(2)]
+    for k in range(3):
+        carry_x = 0.5 * (field_at(0, 1, 0, k) + field_at(0, 1, 1, k))
+        carry_y = 0.5 * (field_at(1, 1, 0, k) + field_at(1, 0, 0, k))
+        for q in range(2):
+            flows = []
+            for d in range(2):
+                taps = (
+                    [field_at(q, 1, down, k) for down in (-1, 0, 1, 2)]
+                    if d == 0
+                    else [field_at(q, s, 0, k) for s in (2, 1, 0, -1)]
+                )
+                weights = [
+                    cf[k, (8 * d + 4 * q + s) * 40 : (8 * d + 4 * q + s) * 40 + 40, :] + b3[8 * d + 4 * q + s]
+                    for s in range(4)
+                ]
+                mean = 0.25 * ((weights[0] + weights[1]) + (weights[2] + weights[3]))
+                total = None
+                for s in range(4):
+                    term = (stencil_base[s] + weights[s] - mean) * taps[s]
+                    total = term if total is None else total + term
+                flows.append((carry_x if d == 0 else carry_y) * total)
+            fx[0, q, k] = flows[0]
+            fx[1, q, k] = flows[1]
+    for q in range(2):
+        along_y = jnp.concatenate([fx[1, q, k, pl.ds(1, 32), :] for k in range(3)], axis=1)
+        along_x = jnp.concatenate(
+            [fx[0, q, k, pl.ds(1, 32), :] - fx[0, q, k, pl.ds(0, 32), :] for k in range(3)], axis=1
+        )
+        here = jnp.concatenate([field_at(q, 1, 1, k, 32) for k in range(3)], axis=1)
+        moved = here - step_ratio * (along_x + along_y - pltpu.roll(along_y, 1, 1))
+        moved = pltpu.roll(moved, 383, 1)
+        for h in range(2):
+            out[q * 2 + h] = moved[:, h * 128 : h * 128 + 128]
+
+
+def star_fields(u_field, v_field, layers):
     w_first, b_first, w_second, b_second, w_third, b_third = layers
-    inputs = lax.dynamic_slice(
-        features, (0, top_row, left_col), (features.shape[0], height + 6, breadth + 6)
+    whole = pl.BlockSpec(memory_space=pltpu.VMEM)
+    return pl.pallas_call(
+        front_kernel,
+        out_shape=jax.ShapeDtypeStruct((4, 32, 128), f32),
+        in_specs=[whole] * 7 + [pl.BlockSpec(memory_space=pltpu.SMEM)],
+        out_specs=whole,
+        scratch_shapes=[
+            pltpu.VMEM((2, 2, 8, 256), f32),
+            pltpu.VMEM((2, 2, 32, 128), f32),
+            pltpu.VMEM((2, 2, 2, 8, 128), f32),
+            pltpu.VMEM((6, 2, 3, 56, 128), f32),
+            pltpu.VMEM((48, 256), f32),
+            pltpu.VMEM((3, 256, 384), bf16),
+            pltpu.VMEM((192, 384), bf16),
+            pltpu.VMEM((2, 10 * PITCH + 16, 128), f32),
+            pltpu.VMEM((9 * PITCH + 384, 256), bf16),
+            pltpu.VMEM((3, 640, 128), f32),
+            pltpu.VMEM((2, 2, 3, 40, 128), f32),
+            pltpu.SemaphoreType.DMA((16,)),
+            pltpu.SemaphoreType.DMA((16,)),
+        ],
+        compiler_params=pltpu.CompilerParams(collective_id=1, has_side_effects=True),
+        name="advect",
+    )(
+        u_field, v_field, jnp.transpose(w_first, (0, 2, 1)), b_first[None], w_second, b_second[None],
+        w_third, b_third,
     )
-    first = jax.nn.relu(convolve(inputs, w_first, b_first, height + 4, breadth + 4)).astype(
-        jnp.bfloat16
-    )
-    second = jax.nn.relu(convolve(first, w_second, b_second, height + 2, breadth + 2)).astype(
-        jnp.bfloat16
-    )
-    return convolve(second, w_third, b_third, height, breadth)
-
-
-def coefficients(features, layers, margin, first_col, breadth):
-    height = features.shape[1] - 2 * margin
-    initial = jnp.zeros((layers[4].shape[1], height, breadth), jnp.float32)
-
-    def advance(position, outputs):
-        start_row = position * block_height
-        piece = predict(
-            features, layers, start_row + margin - 3, margin - 3 + first_col, block_height, breadth
-        )
-        return lax.dynamic_update_slice(outputs, piece, (0, start_row, 0))
-
-    return lax.fori_loop(0, height // block_height, advance, initial)
-
-
-def fluxes(padded, coeff, margin, anchor, height, breadth):
-
-    def sample(shift_down, shift_right):
-        top_row = margin + anchor + shift_down
-        left_col = margin + anchor + shift_right
-        return padded[:, top_row : top_row + height, left_col : left_col + breadth]
-
-    weights = coeff.reshape(2, 2, 4, height, breadth)
-    weights = (
-        jnp.asarray(stencil_base, jnp.float32)[:, None, None]
-        + weights
-        - jnp.mean(weights, axis=2, keepdims=True)
-    )
-    centre = sample(0, 0)
-    east = (
-        weights[0, :, 0] * sample(-1, 0)
-        + weights[0, :, 1] * centre
-        + weights[0, :, 2] * sample(1, 0)
-        + weights[0, :, 3] * sample(2, 0)
-    )
-    north = (
-        weights[1, :, 0] * sample(0, -1)
-        + weights[1, :, 1] * centre
-        + weights[1, :, 2] * sample(0, 1)
-        + weights[1, :, 3] * sample(0, 2)
-    )
-    carry_x = 0.5 * (centre[0] + sample(1, 0)[0])
-    carry_y = 0.5 * (centre[1] + sample(0, 1)[1])
-    return (carry_x * east, carry_y * north)
-
-
-def star_fields(u_field, v_field, layers):
-    field = jnp.stack([u_field, v_field])
-    height, breadth = u_field.shape
-    padded = padded_2(field, (("gx", 1), ("gy", 2)), 3)
-    features = padded.astype(jnp.bfloat16)
-    coeff = coefficients(features, layers, 3, 0, breadth)
-    east_now, north_now = fluxes(padded, coeff, 3, 0, height, breadth)
-    below = from_behind(east_now[:, -1:, :], "gx", 1)
-    beside = from_behind(north_now[:, :, -1:], "gy", 1)
-    east_before = jnp.concatenate([below, east_now[:, :-1]], axis=1)
-    north_before = jnp.concatenate([beside, north_now[:, :, :-1]], axis=2)
-    return field - step_ratio * (east_now - east_before + north_now - north_before)
 
 
 def split_bf16(table):
@@ -238,12 +349,9 @@
         pltpu.make_async_copy(like, like, sem).wait()
 
     for c in range(2):
-        for h in range(2):
-            st[c * 2 + h] = star[c, :, h * 128 : h * 128 + 128]
-    for c in range(2):
         for r in range(2):
             for h in range(2):
-                s1[:, c * 4 + r * 2 + h, :] = st[c * 2 + h, pl.ds(r, 16, stride=2), :]
+                s1[:, c * 4 + r * 2 + h, :] = star[c * 2 + h, pl.ds(r, 16, stride=2), :]
     send_y(0, s1, r1)
 
     shape = (32, 256)
@@ -366,7 +474,7 @@
     for c in range(2):
         for h in range(2):
             lanes = slice(h * 128, h * 128 + 128)
-            out[c, :, lanes] = 0.5 * star[c, :, lanes] + st[c * 2 + h]
+            out[c, :, lanes] = 0.5 * star[c * 2 + h] + st[c * 2 + h]
 
     for stage, buffer in ((0, s1), (2, s3), (3, s4), (5, s6)):
         wait_for(ssem.at[stage], buffer.at[pl.ds(0, GY - 1)])

time: 131 us -> 75.6 us (0.58)
  matrix products: 33.7 us -> 0 us
  Pallas kernels: 48.2 us -> 73.3 us
  starting transfers between devices: 23.7 us -> 0 us
  waiting for transfers between devices: 15.1 us -> 0 us
  other arithmetic: 5.24 us -> 0 us
    dot_general x108 -> x0, matrix products: 33.7 us -> none  [convolve(): jnp.einsum('oc,chw->ohw', kernel[tap_index], window, preferred_element_ty...]
    pallas_call x0 -> x1, Pallas kernels: none -> 29.5 us  [star_fields(): pl.pallas_call(front_kernel, out_shape=jax.ShapeDtypeStruct((4, 32, 128),...]
    ppermute x6 -> x0, starting transfers between devices: 23.7 us -> none  [the longest x2 16 us: padded_2(): after = lax.ppermute(first, axis, down)]
    ppermute x6 -> x0, waiting for transfers between devices: 15.1 us -> none  [the longest x2 8.75 us: padded_2(): before = lax.ppermute(last, axis, up)]
    pallas_call x1, Pallas kernels: 48.2 us -> 43.8 us  [project(): pl.pallas_call(spectral_kernel, out_shape=jax.ShapeDtypeStruct((2, 32, 25...]
    concatenate x4 -> x0, other arithmetic: 1.68 us -> none  [padded_2(): value = jnp.concatenate([before, value, after], axis=dim)]
    another operation x4 -> x0, other arithmetic: 1.64 us -> none  [the longest x1 0.84 us: star_fields(): field = jnp.stack([u_field, v_field])]
  transfers between devices with their start and end apart: 6 -> 0, of which waited for: 3 -> 0; matrix products, arithmetic and copies ran while one was open for 2% -> 0% of each run, Pallas kernels for 0% -> 0%
where the time goes in v2:
time: 75.6 us; the launch traced here: 75.4 us
  Pallas kernels  73.3 us (97%)
  local copies, waits for them, and re-layouts  1.4 us (2%)
    pallas_call x1, Pallas kernels, project(): pl.pallas_call(spectral_kernel, out_shape=jax.ShapeDtypeStruct((2, 32, 25...  43.8 us
    pallas_call x1, Pallas kernels, star_fields(): pl.pallas_call(front_kernel, out_shape=jax.ShapeDtypeStruct((4, 32, 128),...  29.5 us

profile of v2, /device:TPU:1, one launch (start us, length us, event | category | flops | bytes accessed | tf_op | source)
XLA Modules:
  0.0 75.4 jit_solution(7617737801186914554)
XLA Ops:
  0.6 29.5 %advect.1.star = f32[4,32,128]{2,1,0:T(8,128)} custom-call(f32[32,256]{1,0:T(8,128)} %u.1, f32[32,256]{1,0:T(8,128)} %v.1, bf16[9,2,64]{2,1,0:T(2,128)(2,1)} %bitcast.7, f32[1,64]{1,0:T(1,128)} %bitcast.8, bf16[9,64,64]{2,1,0:T(8,128)(2,1)} %w2.1, f32[1,64]{1,0:T(1,128)} %bitcast.9, bf16[9,16,64]{2,1,0:T(8,128)(2,1)} %w3.1, f32[16]{0:T(128)} %b3.1), custom_call_target="tpu_custom_call" | custom-call | tf_op jit(solution)/shard_map/advect/pallas_call | solution.py:212
  30.1 43.8 %spectral.1 = f32[2,32,256]{2,1,0:T(8,128)} custom-call(f32[4,32,128]{2,1,0:T(8,128)} %advect.1.star, bf16[2,32,96]{2,1,0:T(8,128)(2,1)} %constant.10.clone.t_a, bf16[2,512,512]{2,1,0:T(8,128)(2,1)} %constant.11.clone.t_b, f32[2,16,256]{2,1,0:T(8,128)} %constant.12.clone.tw, bf16[4,64,192]{2,1,0:T(8,128)(2,1)} %constant.13.clone.t_s, ...), custom_call_target="tpu_custom_call" | custom-call | tf_op jit(solution)/shard_map/spectral/pallas_call | solution.py:491
  74.0 1.4 %slice_bitcast_fusion = (f32[32,256]{1,0:T(8,128)}, f32[32,256]{1,0:T(8,128)}) fusion(f32[2,32,256]{2,1,0:T(8,128)} %spectral.1), kind=kLoop, calls=%fused_computation | loop fusion | bytes 131072 | tf_op jit(solution)/shard_map/squeeze | solution.py:511

commit v3 on v1

v3 whole, which is shorter than its diff:
```python
import functools
import math

import jax
import jax.numpy as jnp
import ml_dtypes
import numpy as np
from jax import lax
from jax.experimental import pallas as pl
from jax.experimental.pallas import tpu as pltpu
from jax.sharding import PartitionSpec as P

step_ratio = 0.4
stencil_base = (-0.0625, 0.5625, 0.5625, -0.0625)
GX = 32
GY = 16
NX = 1024
NY = 4096
PITCH = 272
SHIFTS = (4, 3, 2, 1, 0, -1)
MESH = pl.DeviceIdType.MESH
f32 = jnp.float32
bf16 = jnp.bfloat16


def split_bf16(table):
    hi = table.astype(np.float32).astype(ml_dtypes.bfloat16)
    lo = (table - hi.astype(np.float64)).astype(np.float32).astype(ml_dtypes.bfloat16)
    return hi, lo


def real_left(matrix):
    return np.block([[matrix.real, -matrix.imag], [matrix.imag, matrix.real]])


def triple_left(table):
    hi, lo = split_bf16(table)
    return np.concatenate([hi, hi, lo], axis=1)


def root(product, whole):
    return np.exp(-2j * np.pi * (product % whole) / whole)


@functools.cache
def tables():
    n8, n16, n32, n256 = (np.arange(n) for n in (8, 16, 32, 256))
    paired = np.concatenate([4 * n8 + t for t in range(4)])
    sign = np.concatenate([np.ones(16), -np.ones(16)])
    halves = [n8, n8 + 8]
    t_a = np.stack([triple_left(real_left(root(np.outer(k, n16), 16)) * sign[None, :]) for k in halves])
    t_a2 = np.stack([triple_left(real_left(root(np.outer(n16, k), 16)) * sign[:, None]) for k in halves])
    mid = root(np.outer(n256, n256), 256)
    t_b = np.stack(split_bf16(np.block([[mid.real, mid.imag], [-mid.imag, mid.real]])))
    turn = [root(np.outer(k, n256), 4096) for k in halves]
    tw = np.stack([np.stack([w.real, w.imag]) for w in turn]).astype(np.float32)
    t_s = np.stack(
        [
            triple_left(real_left(root(np.outer(paired, n32), 32))),
            triple_left(real_left(root(np.outer(n32, paired), 32))),
        ]
    )
    twr = np.zeros((8, 32, 8), np.float32)
    for r in range(4):
        row = root(np.outer(4 * n8 + r, paired), 1024)
        twr[:, :, 2 * r] = row.real
        twr[:, :, 2 * r + 1] = row.imag
    return t_a, t_a2, t_b, tw, t_s, twr


def triple(value):
    hi = value.astype(bf16)
    lo = (value - hi.astype(f32)).astype(bf16)
    return jnp.concatenate([hi, lo, hi], axis=0)


def left_product(table, value):
    return jnp.dot(table, triple(value), preferred_element_type=f32)


def right_product(value, t_b):
    rows = value.shape[0]
    hi = value.astype(bf16)
    lo = (value - hi.astype(f32)).astype(bf16)
    both = jnp.dot(jnp.concatenate([hi, lo], axis=0), t_b[0], preferred_element_type=f32)
    return both[:rows] + both[rows:] + jnp.dot(hi, t_b[1], preferred_element_type=f32)


def nt(left, right):
    return lax.dot_general(left, right, (((1,), (1,)), ((), ())), preferred_element_type=f32)


def swap_halves(low, high, lane):
    first = lane < 64
    return jnp.where(first, low, pltpu.roll(high, 64, 1)), jnp.where(first, pltpu.roll(low, 64, 1), high)


def far_first(step, size):
    half = (step + 1) // 2
    return size // 2 + half - 2 * half * (step % 2)


def wait_for(sem, like):
    pltpu.make_async_copy(like, like, sem).wait()


def kernel(names, *refs):
    r = dict(zip(names, refs))
    a = lax.axis_index("gx")
    b = lax.axis_index("gy")
    y_at, x_hi = b // 2, b % 2

    local = []
    for n, name in enumerate(("u", "v", "w1", "w2", "w3", "b1", "b2", "b3", "t_a", "t_a2", "t_b", "tw", "t_s", "twr")):
        copy = pltpu.make_async_copy(r[name + "_hbm"], r[name], r["lsem"].at[n])
        copy.start()
        local.append(copy)
    u, v = r["u"], r["v"]

    moves = [(dx, dy) for dx in (-1, 0, 1) for dy in (-1, 0, 1) if (dx, dy) != (0, 0)]

    def at(dx, dy):
        return {"gx": (a + dx + GX) % GX, "gy": (b + dy + GY) % GY}

    barrier = pltpu.get_barrier_semaphore()
    for dx, dy in moves:
        if dx and dy:
            pl.semaphore_signal(barrier, inc=1, device_id=at(dx, dy), device_id_type=MESH)

    def greet_y(step, _):
        peer = (b + far_first(step, GY)) % GY
        pl.semaphore_signal(barrier, inc=1, device_id={"gy": peer}, device_id_type=MESH)
        return 0

    def greet_x(step, _):
        peer = (a + far_first(step, GX)) % GX
        pl.semaphore_signal(barrier, inc=1, device_id={"gx": peer}, device_id_type=MESH)
        return 0

    lax.fori_loop(0, GY - 1, greet_y, 0)
    lax.fori_loop(0, GX - 1, greet_x, 0)
    local[0].wait()
    local[1].wait()
    pl.semaphore_wait(barrier, GX + GY + 2)

    copies = []
    for n, (dx, dy) in enumerate(moves):
        rows = {-1: slice(0, 8), 0: slice(0, 32), 1: slice(24, 32)}[dx]
        cols = {-1: slice(0, 128), 0: slice(0, 256), 1: slice(128, 256)}[dy]
        for c, field in enumerate((u, v)):
            if dx and dy:
                dst = r["corner_in"].at[(dx + 1) // 2, (dy + 1) // 2, c]
            elif dx:
                dst = r["rows_in"].at[(dx + 1) // 2, c]
            else:
                dst = r["cols_in"].at[(dy + 1) // 2, c]
            copy = pltpu.make_async_remote_copy(
                field.at[rows, cols], dst, r["hssem"].at[2 * n + c], r["hrsem"].at[2 * n + c],
                device_id=at(dx, dy), device_id_type=MESH,
            )
            copy.start()
            copies.append(copy)

    k1, k2, k3, x1, x2, fs, cf = (r[n] for n in ("k1", "k2", "k3", "x1", "x2", "fs", "cf"))
    k1[...] = jnp.zeros_like(k1)
    k2[...] = jnp.zeros_like(k2)
    k3[...] = jnp.zeros_like(k3)
    for copy in local[2:]:
        copy.wait()
    w1, w2, w3, b3 = (r[n] for n in ("w1", "w2", "w3", "b3"))
    for dj in range(3):
        for dr in range(3):
            tap = 3 * dr + dj
            for o in range(5):
                x = o + dr
                row = dj * 80 + o * 16
                k3[row : row + 16, x * 64 : x * 64 + 64] = w3[tap]
                if o == 4:
                    continue
                for c in range(2):
                    row = (dj * 2 + c) * 8 + x
                    k1[row : row + 1, o * 64 : o * 64 + 64] = w1[tap, c : c + 1, :].astype(f32)
                k2[dj, o * 64 : o * 64 + 64, x * 64 : x * 64 + 64] = w2[tap]
    bias1 = jnp.concatenate([r["b1"][...]] * 4, axis=1)
    bias2 = jnp.concatenate([r["b2"][...]] * 4, axis=1)
    x1[:, pl.ds(10 * PITCH, 16), :] = jnp.zeros((2, 16, 128), f32)
    x2[pl.ds(9 * PITCH, 384), :] = jnp.zeros((384, 256), bf16)

    shape = (32, 256)
    m2 = lax.broadcasted_iota(jnp.int32, shape, 0)
    lane = lax.broadcasted_iota(jnp.int32, shape, 1)
    kx = 4 * y_at + lane // 64 + 32 * m2
    ky = a // 4 + 8 * x_hi + 16 * ((a % 4) * 64 + lane % 64)
    wx = jnp.where(kx >= NX // 2, kx - NX, kx).astype(f32) * (2.0 * math.pi / NX)
    wy = jnp.where(ky >= NY // 2, ky - NY, ky).astype(f32) * (2.0 * math.pi / NY)
    den = wx * wx + wy * wy
    origin = (kx == 0) & (ky == 0)
    den = jnp.where(origin, 1.0, den)
    scale = 1.0 / (NX * NY)
    share = scale / den
    g_re = 0.5 * (wy * wy - wx * wx) * share
    g_im = jnp.where((kx == NX // 2) != (ky == NY // 2), 0.0, -(wx * wy) * share)
    r["gain"][0] = jnp.where(origin, 0.5 * scale, g_re)
    r["gain"][1] = jnp.where(origin, -0.5 * scale, g_re)
    r["gain"][2] = g_im

    for copy in copies:
        copy.wait_recv()

    lane = lax.broadcasted_iota(jnp.int32, (8, 128), 1)
    for c, field in enumerate((u, v)):
        for g in range(6):
            if g in (0, 5):
                e = 1 if g == 0 else 0
                corner, rows_in = r["corner_in"], r["rows_in"]
                tiles = [corner[e, 1, c], rows_in[e, c, :, 0:128], rows_in[e, c, :, 128:256], corner[e, 0, c]]
            else:
                rows = slice(g * 8 - 8, g * 8)
                cols_in = r["cols_in"]
                tiles = [cols_in[1, c, rows, :], field[rows, 0:128], field[rows, 128:256], cols_in[0, c, rows, :]]
            for n, s in enumerate(SHIFTS):
                turned = [pltpu.roll(tile, s % 128, 1) if s else tile for tile in tiles]
                for k in range(3):
                    if s > 0:
                        value = jnp.where(lane < s, turned[k], turned[k + 1])
                    elif s < 0 and k < 2:
                        value = jnp.where(lane >= 128 + s, turned[k + 2], turned[k + 1])
                    else:
                        value = turned[k + 1]
                    fs[n, c, k, g * 8 : g * 8 + 8, :] = value

    first_weights = k1[...].astype(bf16)

    def layer_1(i, _):
        patch = jnp.concatenate(
            [
                jnp.concatenate([fs[dj, c, k, pl.ds(4 * i + 4, 8), :] for k in range(3)], axis=1)
                for dj in range(3)
                for c in range(2)
            ],
            axis=0,
        ).astype(bf16)
        y = lax.dot_general(patch, first_weights, (((0,), (0,)), ((), ())), preferred_element_type=f32)
        y = jnp.maximum(y[:PITCH] + bias1, 0.0)
        start = pl.multiple_of(i * PITCH, 8)
        x1[0, pl.ds(start, PITCH), :] = y[:, :128]
        x1[1, pl.ds(start, PITCH), :] = y[:, 128:]
        return 0

    lax.fori_loop(0, 10, layer_1, 0)

    chunk = 3 * PITCH

    def layer_2(i, _):
        start = i * chunk

        def piece(half, offset):
            return x1[half, pl.ds(start + offset, chunk), :].astype(bf16)

        y = None
        for dj in range(3):
            left = jnp.concatenate([piece(0, dj), piece(1, dj)], axis=1)
            term = nt(left, k2[dj, :, 0:256])
            y = term if y is None else y + term
        left = jnp.concatenate([piece(0, PITCH), piece(0, PITCH + 1)], axis=1)
        y = y + nt(left, jnp.concatenate([k2[0, :, 256:384], k2[1, :, 256:384]], axis=1))
        y = y + nt(piece(0, PITCH + 2), k2[2, :, 256:384])
        x2[pl.ds(pl.multiple_of(start, 16), chunk), :] = jnp.maximum(y + bias2, 0.0).astype(bf16)
        return 0

    lax.fori_loop(0, 3, layer_2, 0)

    s1, r1, st = r["s1"], r["r1"], r["st"]
    ssem, rsem = r["ssem"], r["rsem"]

    def layer_3(step, _):
        i = (y_at + far_first(step, 8)) % 8
        start = pl.multiple_of(i * PITCH, 16)
        after = pl.multiple_of((i + 1) * PITCH, 16)
        y = nt(k3[:, 0:256], x2[pl.ds(start, 384), :]) + nt(k3[:, 256:448], x2[pl.ds(after, 384), 0:192])
        y = y[0:80] + pltpu.roll(y[80:160], 383, 1) + pltpu.roll(y[160:240], 382, 1)
        for o in range(5):
            for k in range(3):
                cf[k, pl.ds(o, 16, stride=8), :] = y[o * 16 : o * 16 + 16, k * 128 : k * 128 + 128]

        def field_at(c, s, down, k):
            return fs[SHIFTS.index(s), c, k, pl.ds(4 * i + 7 + down, 8), :]

        flows = [[[], []] for _ in range(2)]
        for k in range(3):
            carry = (
                0.5 * (field_at(0, 1, 0, k) + field_at(0, 1, 1, k)),
                0.5 * (field_at(1, 1, 0, k) + field_at(1, 0, 0, k)),
            )
            for q in range(2):
                for d in range(2):
                    if d == 0:
                        taps = [field_at(q, 1, down, k) for down in (-1, 0, 1, 2)]
                    else:
                        taps = [field_at(q, s, 0, k) for s in (2, 1, 0, -1)]
                    base = 8 * d + 4 * q
                    weights = [cf[k, (base + s) * 8 : (base + s) * 8 + 8, :] + b3[base + s] for s in range(4)]
                    mean = 0.25 * ((weights[0] + weights[1]) + (weights[2] + weights[3]))
                    total = None
                    for s in range(4):
                        term = (stencil_base[s] + weights[s] - mean) * taps[s]
                        total = term if total is None else total + term
                    flows[d][q].append(carry[d] * total)
        for q in range(2):
            along_x = jnp.concatenate(flows[0][q], axis=1)
            along_y = jnp.concatenate(flows[1][q], axis=1)
            change = pltpu.roll(along_x + (along_y - pltpu.roll(along_y, 1, 1)), 7, 0) - along_x
            here = jnp.concatenate([field_at(q, 1, 1, k) for k in range(3)], axis=1)
            moved = pltpu.roll(here - step_ratio * change, 383, 1)
            for h in range(2):
                value = moved[0:4, h * 128 : h * 128 + 128]
                st[q * 2 + h, pl.ds(4 * i, 4), :] = value
                s1[i, q * 8 + h * 4 : q * 8 + h * 4 + 4, :] = value
        for other in range(2):
            peer = 2 * i + other

            @pl.when(peer != b)
            def _():
                pltpu.make_async_remote_copy(
                    s1.at[i], r1.at[b], ssem.at[0], rsem.at[0], device_id={"gy": peer}, device_id_type=MESH
                ).start()

        return 0

    lax.fori_loop(0, 8, layer_3, 0)
    r1[b] = s1[y_at]

    def send(stage, axis, size, peer_of, src_of, dst):
        def go(step, _):
            peer = peer_of(step)
            pltpu.make_async_remote_copy(
                src_of(peer), dst, ssem.at[stage], rsem.at[stage], device_id={axis: peer}, device_id_type=MESH
            ).start()
            return 0

        lax.fori_loop(0, size - 1, go, 0)

    def x_peer(step):
        return (a + far_first(step, GX)) % GX

    def y_peer(step):
        return 2 * ((y_at + far_first(step, 8)) % 8) + x_hi

    def all_y_peer(step):
        return (b + far_first(step, GY)) % GY

    wait_for(rsem.at[0], r1.at[pl.ds(0, GY - 1)])

    tr, ti = r["tw"][x_hi, 0], r["tw"][x_hi, 1]
    x = jnp.concatenate(
        [
            jnp.concatenate([r1[:, c * 8 + h * 4 + i, :] for i in range(4) for h in range(2)], axis=1)
            for c in range(2)
        ],
        axis=0,
    )
    y = left_product(r["t_a"][x_hi], x)
    lines = []
    for i in range(4):
        yr, yi = y[:8, i * 256 : i * 256 + 256], y[8:, i * 256 : i * 256 + 256]
        lines.append(jnp.concatenate([yr * tr - yi * ti, yr * ti + yi * tr], axis=1))
    o = right_product(jnp.concatenate(lines, axis=0), r["t_b"])
    s2, r2 = r["s2"], r["r2"]
    for c in range(2):
        for rp in range(2):
            for h in range(2):
                cols = slice(c * 256 + h * 128, c * 256 + h * 128 + 128)
                pair = swap_halves(o[rp * 16 : rp * 16 + 8, cols], o[rp * 16 + 8 : rp * 16 + 16, cols], lane)
                for low in range(2):
                    s2[:, 2 * h + low, c * 2 + rp, :] = pair[low]
    send(1, "gx", GX, x_peer, lambda peer: s2.at[peer // 4, peer % 4], r2.at[a])
    r2[a] = s2[a // 4, a % 4]
    wait_for(rsem.at[1], r2.at[pl.ds(0, GX - 1)])

    x = jnp.concatenate(
        [jnp.concatenate([r2[:, c * 2 + rp, :] for rp in range(2)], axis=1) for c in range(2)], axis=0
    )
    y = left_product(r["t_s"][0], x)
    column = r["twr"][y_at]
    wide = lax.broadcasted_iota(jnp.int32, (32, 128), 1) < 64
    turns = [
        [jnp.where(wide, column[:, 4 * rp + c : 4 * rp + c + 1], column[:, 4 * rp + 2 + c : 4 * rp + 3 + c]) for c in range(2)]
        for rp in range(2)
    ]
    s3, r3 = r["s3"], r["r3"]
    for rp in range(2):
        cr, ci = turns[rp]
        yr, yi = y[:32, rp * 128 : rp * 128 + 128], y[32:, rp * 128 : rp * 128 + 128]
        for c, value in enumerate((yr * cr - yi * ci, yr * ci + yi * cr)):
            for tp in range(2):
                pair = swap_halves(value[tp * 16 : tp * 16 + 8], value[tp * 16 + 8 : tp * 16 + 16], lane)
                for low in range(2):
                    s3[:, c * 8 + (2 * rp + low) * 2 + tp, :] = pair[low]
    send(2, "gy", 8, y_peer, lambda peer: s3.at[peer // 2], r3.at[y_at])
    r3[y_at] = s3[y_at]
    wait_for(rsem.at[2], r3.at[pl.ds(0, 7)])
    x = jnp.concatenate(
        [
            jnp.concatenate([r3[:, c * 8 + i * 2 + tp, :] for tp in range(2)], axis=1)
            for c in range(2)
            for i in range(4)
        ],
        axis=0,
    )
    y = left_product(r["t_s"][1], x)
    yr, yi = y[:32], y[32:]

    gain = r["gain"]
    q = jnp.concatenate([gain[0] * yr - gain[2] * yi, -(gain[1] * yi + gain[2] * yr)], axis=0)

    y = left_product(r["t_s"][0], q)
    s4, r4 = r["s4"], r["r4"]
    for c in range(2):
        for i in range(4):
            for tp in range(2):
                row = c * 32 + i * 8
                s4[:, c * 8 + i * 2 + tp, :] = y[row : row + 8, tp * 128 : tp * 128 + 128]
    send(3, "gy", 8, y_peer, lambda peer: s4.at[peer // 2], r4.at[y_at])
    r4[y_at] = s4[y_at]
    wait_for(rsem.at[3], r4.at[pl.ds(0, 7)])
    halves = [[], []]
    for rp in range(2):
        cr, ci = turns[rp]
        parts = []
        for c in range(2):
            rows = []
            for tp in range(2):
                rows += swap_halves(r4[:, c * 8 + 4 * rp + tp, :], r4[:, c * 8 + 4 * rp + 2 + tp, :], lane)
            parts.append(jnp.concatenate(rows, axis=0))
        yr, yi = parts
        halves[0].append(yr * cr - yi * ci)
        halves[1].append(yr * ci + yi * cr)
    x = jnp.concatenate([jnp.concatenate(half, axis=1) for half in halves], axis=0)
    y = left_product(r["t_s"][1], x)
    s5, r5 = r["s5"], r["r5"]
    for c in range(2):
        for rp in range(2):
            s5[:, c * 2 + rp, :] = y[c * 32 : c * 32 + 32, rp * 128 : rp * 128 + 128]
    send(4, "gx", GX, x_peer, lambda peer: s5.at[peer], r5.at[a // 4, a % 4])
    r5[a // 4, a % 4] = s5[a]
    wait_for(rsem.at[4], s5.at[pl.ds(0, GX - 1)])
    lines = [[None] * 4 for _ in range(4)]
    for c in range(2):
        for rp in range(2):
            for h in range(2):
                pair = swap_halves(r5[:, 2 * h, c * 2 + rp, :], r5[:, 2 * h + 1, c * 2 + rp, :], lane)
                for low in range(2):
                    lines[2 * rp + low][c * 2 + h] = pair[low]
    x = jnp.concatenate([jnp.concatenate(line, axis=1) for line in lines], axis=0)
    o = right_product(x, r["t_b"])
    lines = [[], []]
    for i in range(4):
        yr, yi = o[i * 8 : i * 8 + 8, :256], o[i * 8 : i * 8 + 8, 256:]
        lines[0].append(yr * tr - yi * ti)
        lines[1].append(yr * ti + yi * tr)
    x = jnp.concatenate([jnp.concatenate(line, axis=1) for line in lines], axis=0)
    y = left_product(r["t_a2"][x_hi], x)
    s6, r6 = r["s6"], r["r6"]
    for c in range(2):
        for i in range(4):
            for h in range(2):
                at_lane = i * 256 + h * 128
                s6[:, c * 8 + h * 4 + i, :] = y[c * 16 : c * 16 + 16, at_lane : at_lane + 128]
    send(5, "gy", GY, all_y_peer, lambda peer: s6.at[peer], r6.at[y_at, x_hi])
    r6[y_at, x_hi] = s6[b]
    wait_for(rsem.at[5], s6.at[pl.ds(0, GY - 1)])
    back = r["back"]
    for c, out in enumerate((r["u_next"], r["v_next"])):
        for h in range(2):
            for i in range(4):
                index = c * 8 + h * 4 + i
                back[pl.ds(i, 8, stride=4), :] = r6[:, 0, index, :] + r6[:, 1, index, :]
            out[:, h * 128 : h * 128 + 128] = 0.5 * st[c * 2 + h] + back[...]

    for copy in copies:
        copy.wait_send()
    for stage, like in (
        (0, r1.at[pl.ds(0, GY - 1)]),
        (1, r2.at[pl.ds(0, GX - 1)]),
        (2, s3.at[pl.ds(0, 7)]),
        (3, s4.at[pl.ds(0, 7)]),
        (4, s5.at[pl.ds(0, GX - 1)]),
        (5, s6.at[pl.ds(0, GY - 1)]),
    ):
        wait_for(ssem.at[stage], like)


def on_device(u_field, v_field, w_first, b_first, w_second, b_second, w_third, b_third):
    inputs = {
        "u": u_field, "v": v_field, "w1": jnp.transpose(w_first, (0, 2, 1)), "w2": w_second, "w3": w_third,
        "b1": b_first[None], "b2": b_second[None], "b3": b_third,
    }
    inputs.update(zip(("t_a", "t_a2", "t_b", "tw", "t_s", "twr"), (jnp.asarray(t) for t in tables())))
    scratch = {
        name: (pltpu.SMEM if name == "b3" else pltpu.VMEM)(value.shape, value.dtype)
        for name, value in inputs.items()
    }
    scratch |= {
        "rows_in": pltpu.VMEM((2, 2, 8, 256), f32),
        "cols_in": pltpu.VMEM((2, 2, 32, 128), f32),
        "corner_in": pltpu.VMEM((2, 2, 2, 8, 128), f32),
        "fs": pltpu.VMEM((6, 2, 3, 56, 128), f32),
        "k1": pltpu.VMEM((48, 256), f32),
        "k2": pltpu.VMEM((3, 256, 384), bf16),
        "k3": pltpu.VMEM((240, 512), bf16),
        "x1": pltpu.VMEM((2, 10 * PITCH + 16, 128), f32),
        "x2": pltpu.VMEM((9 * PITCH + 384, 256), bf16),
        "cf": pltpu.VMEM((3, 128, 128), f32),
        "st": pltpu.VMEM((4, 32, 128), f32),
        "back": pltpu.VMEM((32, 128), f32),
        "gain": pltpu.VMEM((3, 32, 256), f32),
        "s1": pltpu.VMEM((8, 16, 128), f32),
        "r1": pltpu.VMEM((16, 16, 128), f32),
        "s2": pltpu.VMEM((8, 4, 4, 128), f32),
        "r2": pltpu.VMEM((32, 4, 128), f32),
        "s3": pltpu.VMEM((8, 16, 128), f32),
        "r3": pltpu.VMEM((8, 16, 128), f32),
        "s4": pltpu.VMEM((8, 16, 128), f32),
        "r4": pltpu.VMEM((8, 16, 128), f32),
        "s5": pltpu.VMEM((32, 4, 128), f32),
        "r5": pltpu.VMEM((8, 4, 4, 128), f32),
        "s6": pltpu.VMEM((16, 16, 128), f32),
        "r6": pltpu.VMEM((8, 2, 16, 128), f32),
        "lsem": pltpu.SemaphoreType.DMA((len(inputs),)),
        "hssem": pltpu.SemaphoreType.DMA((16,)),
        "hrsem": pltpu.SemaphoreType.DMA((16,)),
        "ssem": pltpu.SemaphoreType.DMA((6,)),
        "rsem": pltpu.SemaphoreType.DMA((6,)),
    }
    names = [name + "_hbm" for name in inputs] + ["u_next", "v_next"] + list(scratch)
    block = jax.ShapeDtypeStruct((32, 256), f32)
    return pl.pallas_call(
        functools.partial(kernel, names),
        out_shape=(block, block),
        in_specs=[pl.BlockSpec(memory_space=pltpu.HBM)] * len(inputs),
        out_specs=(pl.BlockSpec(memory_space=pltpu.VMEM),) * 2,
        scratch_shapes=list(scratch.values()),
        compiler_params=pltpu.CompilerParams(collective_id=0, has_side_effects=True),
        name="step",
    )(*inputs.values())


def solution(mesh):
    return jax.shard_map(
        on_device,
        mesh=mesh,
        in_specs=(P("gx", "gy"), P("gx", "gy"), P(), P(), P(), P(), P(), P()),
        out_specs=(P("gx", "gy"), P("gx", "gy")),
        check_vma=False,
    )
```

time: 131 us -> 66 us (0.50)
  matrix products: 33.7 us -> 0 us
  starting transfers between devices: 23.7 us -> 0 us
  waiting for transfers between devices: 15.1 us -> 0 us
  Pallas kernels: 48.2 us -> 63.2 us
  other arithmetic: 5.24 us -> 0 us
    dot_general x108 -> x0, matrix products: 33.7 us -> none  [convolve(): jnp.einsum('oc,chw->ohw', kernel[tap_index], window, preferred_element_ty...]
    ppermute x6 -> x0, starting transfers between devices: 23.7 us -> none  [the longest x2 16 us: padded_2(): after = lax.ppermute(first, axis, down)]
    ppermute x6 -> x0, waiting for transfers between devices: 15.1 us -> none  [the longest x2 8.75 us: padded_2(): before = lax.ppermute(last, axis, up)]
    pallas_call x1, Pallas kernels: 48.2 us -> 63.2 us  [on_device(): pl.pallas_call(functools.partial(kernel, names), out_shape=(block, block)...]
    concatenate x4 -> x0, other arithmetic: 1.68 us -> none  [padded_2(): value = jnp.concatenate([before, value, after], axis=dim)]
    another operation x4 -> x0, other arithmetic: 1.64 us -> none  [the longest x1 0.84 us: star_fields(): field = jnp.stack([u_field, v_field])]
    unnamed x18 -> x4, local copies, waits for them, and re-layouts: 0.58 us -> 2 us
    squeeze x1 -> x0, local copies, waits for them, and re-layouts: 1.4 us -> none  [on_device(): return (result[0], result[1])]
  transfers between devices with their start and end apart: 6 -> 0, of which waited for: 3 -> 0; matrix products, arithmetic and copies ran while one was open for 2% -> 0% of each run, Pallas kernels for 0% -> 0%
where the time goes in v3:
time: 66 us; the launch traced here: 65.8 us
  Pallas kernels  63.2 us (96%)
  local copies, waits for them, and re-layouts  2 us (3%)
    pallas_call x1, Pallas kernels, on_device(): pl.pallas_call(functools.partial(kernel, names), out_shape=(block, block)...  63.2 us
    unnamed x4, local copies, waits for them, and re-layouts  2 us

profile of v3, /device:TPU:1, one launch (start us, length us, event | category | flops | bytes accessed | tf_op | source)
XLA Modules:
  0.0 65.8 jit_solution(6098559508805060017)
XLA Ops:
  0.6 63.2 %step.1 = (f32[32,256]{1,0:T(8,128)}, f32[32,256]{1,0:T(8,128)}) custom-call(f32[32,256]{1,0:T(8,128)} %refs_0_.1, f32[32,256]{1,0:T(8,128)} %refs_1_.1, bf16[9,2,64]{2,1,0:T(2,128)(2,1)} %bitcast.3, bf16[9,64,64]{2,1,0:T(8,128)(2,1)} %refs_3_.1, bf16[9,16,64]{2,1,0:T(8,128)(2,1)} %refs_4_.1, f32[1,64]{1,0:T(1,128)} %bitcast.4, f32[1,64]{1,0:T(1,128)} %bitcast.5, ...), custom_call_target="tpu_custom_call" | custom-call | tf_op jit(solution)/shard_map/step/pallas_call | solution.py:537
  63.8 0.0 copy-start
  63.8 1.4 %copy.18 = f32[32,256]{1,0:T(8,128)} copy(f32[32,256]{1,0:T(8,128)} %get-tuple-element.4) | data formatting | bytes 65536
  65.2 0.0 copy-done
  65.2 0.6 copy.19
Async XLA Ops:
  63.8 1.4 %copy-start = (f32[32,256]{1,0:T(8,128)S(1)}, f32[32,256]{1,0:T(8,128)}, u32[]{:S(2)}) copy-start(f32[32,256]{1,0:T(8,128)} %get-tuple-element.5) | copy-start | bytes 98308

commit v4 on v3

--- a/solution.py
+++ b/solution.py
@@ -139,33 +139,11 @@
 
     lax.fori_loop(0, GY - 1, greet_y, 0)
     lax.fori_loop(0, GX - 1, greet_x, 0)
-    local[0].wait()
-    local[1].wait()
-    pl.semaphore_wait(barrier, GX + GY + 2)
-
-    copies = []
-    for n, (dx, dy) in enumerate(moves):
-        rows = {-1: slice(0, 8), 0: slice(0, 32), 1: slice(24, 32)}[dx]
-        cols = {-1: slice(0, 128), 0: slice(0, 256), 1: slice(128, 256)}[dy]
-        for c, field in enumerate((u, v)):
-            if dx and dy:
-                dst = r["corner_in"].at[(dx + 1) // 2, (dy + 1) // 2, c]
-            elif dx:
-                dst = r["rows_in"].at[(dx + 1) // 2, c]
-            else:
-                dst = r["cols_in"].at[(dy + 1) // 2, c]
-            copy = pltpu.make_async_remote_copy(
-                field.at[rows, cols], dst, r["hssem"].at[2 * n + c], r["hrsem"].at[2 * n + c],
-                device_id=at(dx, dy), device_id_type=MESH,
-            )
-            copy.start()
-            copies.append(copy)
-
     k1, k2, k3, x1, x2, fs, cf = (r[n] for n in ("k1", "k2", "k3", "x1", "x2", "fs", "cf"))
     k1[...] = jnp.zeros_like(k1)
     k2[...] = jnp.zeros_like(k2)
     k3[...] = jnp.zeros_like(k3)
-    for copy in local[2:]:
+    for copy in local:
         copy.wait()
     w1, w2, w3, b3 = (r[n] for n in ("w1", "w2", "w3", "b3"))
     for dj in range(3):
@@ -186,11 +164,123 @@
     x1[:, pl.ds(10 * PITCH, 16), :] = jnp.zeros((2, 16, 128), f32)
     x2[pl.ds(9 * PITCH, 384), :] = jnp.zeros((384, 256), bf16)
 
+    lane = lax.broadcasted_iota(jnp.int32, (8, 128), 1)
+
+    def surround(groups, arrived):
+        for c, field in enumerate((u, v)):
+            for g in groups:
+                if g in (0, 5):
+                    e = 1 if g == 0 else 0
+                    corner, rows_in = r["corner_in"], r["rows_in"]
+                    tiles = [corner[e, 1, c], rows_in[e, c, :, 0:128], rows_in[e, c, :, 128:256], corner[e, 0, c]]
+                else:
+                    rows = slice(g * 8 - 8, g * 8)
+                    tiles = [field[rows, 0:128], field[rows, 128:256]]
+                    if arrived:
+                        cols_in = r["cols_in"]
+                        tiles = [cols_in[1, c, rows, :], *tiles, cols_in[0, c, rows, :]]
+                    else:
+                        tiles = [tiles[1], *tiles, tiles[0]]
+                for n, s in enumerate(SHIFTS):
+                    turned = [pltpu.roll(tile, s % 128, 1) if s else tile for tile in tiles]
+                    for k in range(3):
+                        if s > 0:
+                            value = jnp.where(lane < s, turned[k], turned[k + 1])
+                        elif s < 0 and k < 2:
+                            value = jnp.where(lane >= 128 + s, turned[k + 2], turned[k + 1])
+                        else:
+                            value = turned[k + 1]
+                        fs[n, c, k, g * 8 : g * 8 + 8, :] = value
+
+    first_weights = k1[...].astype(bf16)
+
+    def patches(i, tiles):
+        return [
+            jnp.concatenate([fs[dj, c, k, pl.ds(4 * i + 4, 8), :] for k in tiles], axis=1)
+            for dj in range(3)
+            for c in range(2)
+        ]
+
+    def first(patch):
+        y = lax.dot_general(
+            patch.astype(bf16), first_weights, (((0,), (0,)), ((), ())), preferred_element_type=f32
+        )
+        return y
+
+    def layer_1(i):
+        y = first(jnp.concatenate(patches(i, range(3)), axis=0))
+        y = jnp.maximum(y[:PITCH] + bias1, 0.0)
+        x1[0, pl.ds(i * PITCH, PITCH), :] = y[:, :128]
+        x1[1, pl.ds(i * PITCH, PITCH), :] = y[:, 128:]
+
+    def layer_1_ends(blocks):
+        wide = lax.broadcasted_iota(jnp.int32, (48, 128), 1) // 8
+        slots = [(i, end) for i in blocks for end in range(2)]
+        packed = jnp.zeros((48, 128), f32)
+        for n, (i, end) in enumerate(slots):
+            patch = jnp.concatenate(patches(i, [2 * end]), axis=0)
+            packed = jnp.where(wide == n, pltpu.roll(patch, 8 * n, 1) if n else patch, packed)
+        y = jnp.maximum(first(packed) + bias1, 0.0)
+        for n, (i, end) in enumerate(slots):
+            at_row = i * PITCH + 256 * end
+            x1[0, pl.ds(at_row, 8), :] = y[8 * n : 8 * n + 8, :128]
+            x1[1, pl.ds(at_row, 8), :] = y[8 * n : 8 * n + 8, 128:]
+
+    def layer_2(stretches):
+        def piece(half, offset):
+            return jnp.concatenate(
+                [x1[half, pl.ds(start + offset, length), :].astype(bf16) for start, length in stretches], axis=0
+            )
+
+        y = None
+        for dj in range(3):
+            left = jnp.concatenate([piece(0, dj), piece(1, dj)], axis=1)
+            term = nt(left, k2[dj, :, 0:256])
+            y = term if y is None else y + term
+        left = jnp.concatenate([piece(0, PITCH), piece(0, PITCH + 1)], axis=1)
+        y = y + nt(left, jnp.concatenate([k2[0, :, 256:384], k2[1, :, 256:384]], axis=1))
+        y = y + nt(piece(0, PITCH + 2), k2[2, :, 256:384])
+        y = jnp.maximum(y + bias2, 0.0).astype(bf16)
+        row = 0
+        for start, length in stretches:
+            x2[pl.ds(start, length), :] = y[row : row + length]
+            row += length
+
+    surround(range(1, 5), False)
+    for i in range(1, 8):
+        layer_1(i)
+
+    def inner(i, _):
+        layer_2([(pl.multiple_of((3 * i + 1) * PITCH, 16), 3 * PITCH)])
+        return 0
+
+    lax.fori_loop(0, 2, inner, 0)
+
+    pl.semaphore_wait(barrier, GX + GY + 2)
+
+    copies = []
+    for n, (dx, dy) in enumerate(moves):
+        rows = {-1: slice(0, 8), 0: slice(0, 32), 1: slice(24, 32)}[dx]
+        cols = {-1: slice(0, 128), 0: slice(0, 256), 1: slice(128, 256)}[dy]
+        for c, field in enumerate((u, v)):
+            if dx and dy:
+                dst = r["corner_in"].at[(dx + 1) // 2, (dy + 1) // 2, c]
+            elif dx:
+                dst = r["rows_in"].at[(dx + 1) // 2, c]
+            else:
+                dst = r["cols_in"].at[(dy + 1) // 2, c]
+            copy = pltpu.make_async_remote_copy(
+                field.at[rows, cols], dst, r["hssem"].at[2 * n + c], r["hrsem"].at[2 * n + c],
+                device_id=at(dx, dy), device_id_type=MESH,
+            )
+            copy.start()
+            copies.append(copy)
+
     shape = (32, 256)
     m2 = lax.broadcasted_iota(jnp.int32, shape, 0)
-    lane = lax.broadcasted_iota(jnp.int32, shape, 1)
-    kx = 4 * y_at + lane // 64 + 32 * m2
-    ky = a // 4 + 8 * x_hi + 16 * ((a % 4) * 64 + lane % 64)
+    cell = lax.broadcasted_iota(jnp.int32, shape, 1)
+    kx = 4 * y_at + cell // 64 + 32 * m2
+    ky = a // 4 + 8 * x_hi + 16 * ((a % 4) * 64 + cell % 64)
     wx = jnp.where(kx >= NX // 2, kx - NX, kx).astype(f32) * (2.0 * math.pi / NX)
     wy = jnp.where(ky >= NY // 2, ky - NY, ky).astype(f32) * (2.0 * math.pi / NY)
     den = wx * wx + wy * wy
@@ -206,83 +296,33 @@
 
     for copy in copies:
         copy.wait_recv()
-
-    lane = lax.broadcasted_iota(jnp.int32, (8, 128), 1)
-    for c, field in enumerate((u, v)):
-        for g in range(6):
-            if g in (0, 5):
-                e = 1 if g == 0 else 0
-                corner, rows_in = r["corner_in"], r["rows_in"]
-                tiles = [corner[e, 1, c], rows_in[e, c, :, 0:128], rows_in[e, c, :, 128:256], corner[e, 0, c]]
-            else:
-                rows = slice(g * 8 - 8, g * 8)
-                cols_in = r["cols_in"]
-                tiles = [cols_in[1, c, rows, :], field[rows, 0:128], field[rows, 128:256], cols_in[0, c, rows, :]]
-            for n, s in enumerate(SHIFTS):
-                turned = [pltpu.roll(tile, s % 128, 1) if s else tile for tile in tiles]
-                for k in range(3):
-                    if s > 0:
-                        value = jnp.where(lane < s, turned[k], turned[k + 1])
-                    elif s < 0 and k < 2:
-                        value = jnp.where(lane >= 128 + s, turned[k + 2], turned[k + 1])
-                    else:
-                        value = turned[k + 1]
-                    fs[n, c, k, g * 8 : g * 8 + 8, :] = value
-
-    first_weights = k1[...].astype(bf16)
-
-    def layer_1(i, _):
-        patch = jnp.concatenate(
-            [
-                jnp.concatenate([fs[dj, c, k, pl.ds(4 * i + 4, 8), :] for k in range(3)], axis=1)
-                for dj in range(3)
-                for c in range(2)
-            ],
-            axis=0,
-        ).astype(bf16)
-        y = lax.dot_general(patch, first_weights, (((0,), (0,)), ((), ())), preferred_element_type=f32)
-        y = jnp.maximum(y[:PITCH] + bias1, 0.0)
-        start = pl.multiple_of(i * PITCH, 8)
-        x1[0, pl.ds(start, PITCH), :] = y[:, :128]
-        x1[1, pl.ds(start, PITCH), :] = y[:, 128:]
-        return 0
-
-    lax.fori_loop(0, 10, layer_1, 0)
-
-    chunk = 3 * PITCH
-
-    def layer_2(i, _):
-        start = i * chunk
-
-        def piece(half, offset):
-            return x1[half, pl.ds(start + offset, chunk), :].astype(bf16)
-
-        y = None
-        for dj in range(3):
-            left = jnp.concatenate([piece(0, dj), piece(1, dj)], axis=1)
-            term = nt(left, k2[dj, :, 0:256])
-            y = term if y is None else y + term
-        left = jnp.concatenate([piece(0, PITCH), piece(0, PITCH + 1)], axis=1)
-        y = y + nt(left, jnp.concatenate([k2[0, :, 256:384], k2[1, :, 256:384]], axis=1))
-        y = y + nt(piece(0, PITCH + 2), k2[2, :, 256:384])
-        x2[pl.ds(pl.multiple_of(start, 16), chunk), :] = jnp.maximum(y + bias2, 0.0).astype(bf16)
-        return 0
-
-    lax.fori_loop(0, 3, layer_2, 0)
+    surround(range(6), True)
+    for i in (0, 8, 9):
+        layer_1(i)
+    layer_1_ends(range(1, 8))
+    layer_2(
+        [(0, PITCH), (7 * PITCH, 2 * PITCH)]
+        + [(i * PITCH + 256 * end, 16) for i in range(1, 7) for end in range(2)]
+    )
 
     s1, r1, st = r["s1"], r["r1"], r["st"]
     ssem, rsem = r["ssem"], r["rsem"]
 
-    def layer_3(step, _):
-        i = (y_at + far_first(step, 8)) % 8
+    def block_of(step):
+        return (y_at + far_first(step, 8)) % 8
+
+    def third(i):
         start = pl.multiple_of(i * PITCH, 16)
         after = pl.multiple_of((i + 1) * PITCH, 16)
-        y = nt(k3[:, 0:256], x2[pl.ds(start, 384), :]) + nt(k3[:, 256:448], x2[pl.ds(after, 384), 0:192])
+        return nt(k3[:, 0:256], x2[pl.ds(start, 384), :]) + nt(k3[:, 256:448], x2[pl.ds(after, 384), 0:192])
+
+    def keep(y):
         y = y[0:80] + pltpu.roll(y[80:160], 383, 1) + pltpu.roll(y[160:240], 382, 1)
         for o in range(5):
             for k in range(3):
                 cf[k, pl.ds(o, 16, stride=8), :] = y[o * 16 : o * 16 + 16, k * 128 : k * 128 + 128]
 
+    def advance(i):
         def field_at(c, s, down, k):
             return fs[SHIFTS.index(s), c, k, pl.ds(4 * i + 7 + down, 8), :]
 
@@ -316,6 +356,8 @@
                 value = moved[0:4, h * 128 : h * 128 + 128]
                 st[q * 2 + h, pl.ds(4 * i, 4), :] = value
                 s1[i, q * 8 + h * 4 : q * 8 + h * 4 + 4, :] = value
+
+    def send_block(i):
         for other in range(2):
             peer = 2 * i + other
 
@@ -325,9 +367,18 @@
                     s1.at[i], r1.at[b], ssem.at[0], rsem.at[0], device_id={"gy": peer}, device_id_type=MESH
                 ).start()
 
+    def layer_3(step, _):
+        y = third(block_of(step + 1))
+        i = block_of(step)
+        advance(i)
+        keep(y)
+        send_block(i)
         return 0
 
-    lax.fori_loop(0, 8, layer_3, 0)
+    keep(third(block_of(0)))
+    lax.fori_loop(0, 7, layer_3, 0)
+    advance(y_at)
+    send_block(y_at)
     r1[b] = s1[y_at]
 
     def send(stage, axis, size, peer_of, src_of, dst):
@@ -470,12 +521,12 @@
     r6[y_at, x_hi] = s6[b]
     wait_for(rsem.at[5], s6.at[pl.ds(0, GY - 1)])
     back = r["back"]
-    for c, out in enumerate((r["u_next"], r["v_next"])):
+    for c in range(2):
         for h in range(2):
             for i in range(4):
                 index = c * 8 + h * 4 + i
                 back[pl.ds(i, 8, stride=4), :] = r6[:, 0, index, :] + r6[:, 1, index, :]
-            out[:, h * 128 : h * 128 + 128] = 0.5 * st[c * 2 + h] + back[...]
+            r["fields_next"][c, :, h * 128 : h * 128 + 128] = 0.5 * st[c * 2 + h] + back[...]
 
     for copy in copies:
         copy.wait_send()
@@ -532,17 +583,17 @@
         "ssem": pltpu.SemaphoreType.DMA((6,)),
         "rsem": pltpu.SemaphoreType.DMA((6,)),
     }
-    names = [name + "_hbm" for name in inputs] + ["u_next", "v_next"] + list(scratch)
-    block = jax.ShapeDtypeStruct((32, 256), f32)
-    return pl.pallas_call(
+    names = [name + "_hbm" for name in inputs] + ["fields_next"] + list(scratch)
+    result = pl.pallas_call(
         functools.partial(kernel, names),
-        out_shape=(block, block),
+        out_shape=jax.ShapeDtypeStruct((2, 32, 256), f32),
         in_specs=[pl.BlockSpec(memory_space=pltpu.HBM)] * len(inputs),
-        out_specs=(pl.BlockSpec(memory_space=pltpu.VMEM),) * 2,
+        out_specs=pl.BlockSpec(memory_space=pltpu.VMEM),
         scratch_shapes=list(scratch.values()),
         compiler_params=pltpu.CompilerParams(collective_id=0, has_side_effects=True),
         name="step",
     )(*inputs.values())
+    return result[0], result[1]
 
 
 def solution(mesh):

time: 66 us -> 61.5 us (0.932)
  Pallas kernels: 63.2 us -> 58.9 us
    pallas_call x1, Pallas kernels: 63.2 us -> 58.9 us  [on_device(): pl.pallas_call(functools.partial(kernel, names), out_shape=jax.ShapeDtype...]
    unnamed x4 -> x0, local copies, waits for them, and re-layouts: 2 us -> none
    squeeze x0 -> x1, local copies, waits for them, and re-layouts: none -> 1.4 us  [on_device(): return (result[0], result[1])]
where the time goes in v4:
time: 61.5 us; the launch traced here: 60.9 us
  Pallas kernels  58.9 us (96%)
  local copies, waits for them, and re-layouts  1.4 us (2%)
  between operations  0.64 us (1%)
    pallas_call x1, Pallas kernels, on_device(): pl.pallas_call(functools.partial(kernel, names), out_shape=jax.ShapeDtype...  58.9 us
    squeeze x1, local copies, waits for them, and re-layouts, on_device(): return (result[0], result[1])  1.4 us

profile of v4, /device:TPU:1, one launch (start us, length us, event | category | flops | bytes accessed | tf_op | source)
XLA Modules:
  0.0 60.9 jit_solution(10077122709443186293)
XLA Ops:
  0.6 58.9 %step.1 = f32[2,32,256]{2,1,0:T(8,128)} custom-call(f32[32,256]{1,0:T(8,128)} %refs_0_.1, f32[32,256]{1,0:T(8,128)} %refs_1_.1, bf16[9,2,64]{2,1,0:T(2,128)(2,1)} %bitcast.7, bf16[9,64,64]{2,1,0:T(8,128)(2,1)} %refs_3_.1, bf16[9,16,64]{2,1,0:T(8,128)(2,1)} %refs_4_.1, f32[1,64]{1,0:T(1,128)} %bitcast.8, f32[1,64]{1,0:T(1,128)} %bitcast.9, f32[16]{0:T(128)} %refs_7_.1, ...), custom_call_target="tpu_custom_call" | custom-call | tf_op jit(solution)/shard_map/step/pallas_call | solution.py:587
  59.5 1.4 %slice_bitcast_fusion = (f32[32,256]{1,0:T(8,128)}, f32[32,256]{1,0:T(8,128)}) fusion(f32[2,32,256]{2,1,0:T(8,128)} %step.1), kind=kLoop, calls=%fused_computation | loop fusion | bytes 131072 | tf_op jit(solution)/shard_map/squeeze | solution.py:596

commit v5 on v4

--- a/solution.py
+++ b/solution.py
@@ -110,6 +110,37 @@
     b = lax.axis_index("gy")
     y_at, x_hi = b // 2, b % 2
 
+    def x_peer(step):
+        z = (a % 16 // 2 + far_first(step // 4, 8)) % 8
+        x_lo = (a // 16 + 1 - step % 4 // 2) % 2
+        return x_lo * 16 + z * 2 + (a + 1 - step % 2) % 2
+
+    def y_peer(step):
+        return 2 * ((y_at + far_first(step, 8)) % 8) + x_hi
+
+    def all_y_peer(step):
+        return 2 * ((y_at + far_first(step // 2, 8)) % 8) + (b + 1 - step % 2) % 2
+
+    moves = [(-1, -1), (-1, 1), (1, -1), (1, 1), (0, -1), (0, 1), (-1, 0), (1, 0)]
+
+    def at(dx, dy):
+        return {"gx": (a + dx + GX) % GX, "gy": (b + dy + GY) % GY}
+
+    barrier = pltpu.get_barrier_semaphore()
+    for dx, dy in moves:
+        if dx and dy:
+            pl.semaphore_signal(barrier, inc=1, device_id=at(dx, dy), device_id_type=MESH)
+
+    def greet_y(step, _):
+        pl.semaphore_signal(barrier, inc=1, device_id={"gy": all_y_peer(step)}, device_id_type=MESH)
+        return 0
+
+    def greet_x(step, _):
+        pl.semaphore_signal(barrier, inc=1, device_id={"gx": x_peer(step)}, device_id_type=MESH)
+        return 0
+
+    lax.fori_loop(0, GY - 1, greet_y, 0)
+    lax.fori_loop(0, GX - 1, greet_x, 0)
     local = []
     for n, name in enumerate(("u", "v", "w1", "w2", "w3", "b1", "b2", "b3", "t_a", "t_a2", "t_b", "tw", "t_s", "twr")):
         copy = pltpu.make_async_copy(r[name + "_hbm"], r[name], r["lsem"].at[n])
@@ -117,33 +148,48 @@
         local.append(copy)
     u, v = r["u"], r["v"]
 
-    moves = [(dx, dy) for dx in (-1, 0, 1) for dy in (-1, 0, 1) if (dx, dy) != (0, 0)]
-
-    def at(dx, dy):
-        return {"gx": (a + dx + GX) % GX, "gy": (b + dy + GY) % GY}
-
-    barrier = pltpu.get_barrier_semaphore()
+    local[0].wait()
+    local[1].wait()
+    lane = lax.broadcasted_iota(jnp.int32, (8, 128), 1)
+
+    cols_out, corner_out = r["cols_out"], r["corner_out"]
+    for e in range(2):
+        tile = slice(e * 128, e * 128 + 128)
+        both = jnp.concatenate([u[:, tile], v[:, tile], jnp.zeros((64, 128), f32)], axis=0)
+        cols_out[e] = jnp.transpose(both)[e * 120 : e * 120 + 8]
+        for d in range(2):
+            rows = slice(d * 24, d * 24 + 8)
+            ends = (u[rows, tile], v[rows, tile])
+            other = pltpu.roll(ends[1], 64, 1)
+            corner_out[d, e] = jnp.where(lane < 64, *((other, ends[0]) if e else (ends[0], other)))
+
+    pl.semaphore_wait(barrier, GX + GY + 2)
+
+    copies = []
+
+    def give(src, dst, dx, dy):
+        n = len(copies)
+        copy = pltpu.make_async_remote_copy(
+            src, dst, r["hssem"].at[n], r["hrsem"].at[n], device_id=at(dx, dy), device_id_type=MESH
+        )
+        copy.start()
+        copies.append(copy)
+
     for dx, dy in moves:
+        d, e = (dx + 1) // 2, (dy + 1) // 2
         if dx and dy:
-            pl.semaphore_signal(barrier, inc=1, device_id=at(dx, dy), device_id_type=MESH)
-
-    def greet_y(step, _):
-        peer = (b + far_first(step, GY)) % GY
-        pl.semaphore_signal(barrier, inc=1, device_id={"gy": peer}, device_id_type=MESH)
-        return 0
-
-    def greet_x(step, _):
-        peer = (a + far_first(step, GX)) % GX
-        pl.semaphore_signal(barrier, inc=1, device_id={"gx": peer}, device_id_type=MESH)
-        return 0
-
-    lax.fori_loop(0, GY - 1, greet_y, 0)
-    lax.fori_loop(0, GX - 1, greet_x, 0)
+            give(corner_out.at[d, e], r["corner_in"].at[d, e], dx, dy)
+        elif dy:
+            give(cols_out.at[e], r["cols_in"].at[e], dx, dy)
+        else:
+            for c, field in enumerate((u, v)):
+                give(field.at[pl.ds(d * 24, 8), :], r["rows_in"].at[d, c], dx, dy)
+
     k1, k2, k3, x1, x2, fs, cf = (r[n] for n in ("k1", "k2", "k3", "x1", "x2", "fs", "cf"))
     k1[...] = jnp.zeros_like(k1)
     k2[...] = jnp.zeros_like(k2)
     k3[...] = jnp.zeros_like(k3)
-    for copy in local:
+    for copy in local[2:]:
         copy.wait()
     w1, w2, w3, b3 = (r[n] for n in ("w1", "w2", "w3", "b3"))
     for dj in range(3):
@@ -164,21 +210,21 @@
     x1[:, pl.ds(10 * PITCH, 16), :] = jnp.zeros((2, 16, 128), f32)
     x2[pl.ds(9 * PITCH, 384), :] = jnp.zeros((384, 256), bf16)
 
-    lane = lax.broadcasted_iota(jnp.int32, (8, 128), 1)
-
-    def surround(groups, arrived):
+
+    def surround(groups, sides):
         for c, field in enumerate((u, v)):
             for g in groups:
                 if g in (0, 5):
                     e = 1 if g == 0 else 0
                     corner, rows_in = r["corner_in"], r["rows_in"]
-                    tiles = [corner[e, 1, c], rows_in[e, c, :, 0:128], rows_in[e, c, :, 128:256], corner[e, 0, c]]
+                    ends = [pltpu.roll(corner[e, n], 64, 1) if c else corner[e, n] for n in range(2)]
+                    tiles = [ends[1], rows_in[e, c, :, 0:128], rows_in[e, c, :, 128:256], ends[0]]
                 else:
                     rows = slice(g * 8 - 8, g * 8)
                     tiles = [field[rows, 0:128], field[rows, 128:256]]
-                    if arrived:
-                        cols_in = r["cols_in"]
-                        tiles = [cols_in[1, c, rows, :], *tiles, cols_in[0, c, rows, :]]
+                    if sides:
+                        near = slice(c * 32 + g * 8 - 8, c * 32 + g * 8)
+                        tiles = [sides[1][near], *tiles, sides[0][near]]
                     else:
                         tiles = [tiles[1], *tiles, tiles[0]]
                 for n, s in enumerate(SHIFTS):
@@ -246,7 +292,7 @@
             x2[pl.ds(start, length), :] = y[row : row + length]
             row += length
 
-    surround(range(1, 5), False)
+    surround(range(1, 5), None)
     for i in range(1, 8):
         layer_1(i)
 
@@ -255,26 +301,6 @@
         return 0
 
     lax.fori_loop(0, 2, inner, 0)
-
-    pl.semaphore_wait(barrier, GX + GY + 2)
-
-    copies = []
-    for n, (dx, dy) in enumerate(moves):
-        rows = {-1: slice(0, 8), 0: slice(0, 32), 1: slice(24, 32)}[dx]
-        cols = {-1: slice(0, 128), 0: slice(0, 256), 1: slice(128, 256)}[dy]
-        for c, field in enumerate((u, v)):
-            if dx and dy:
-                dst = r["corner_in"].at[(dx + 1) // 2, (dy + 1) // 2, c]
-            elif dx:
-                dst = r["rows_in"].at[(dx + 1) // 2, c]
-            else:
-                dst = r["cols_in"].at[(dy + 1) // 2, c]
-            copy = pltpu.make_async_remote_copy(
-                field.at[rows, cols], dst, r["hssem"].at[2 * n + c], r["hrsem"].at[2 * n + c],
-                device_id=at(dx, dy), device_id_type=MESH,
-            )
-            copy.start()
-            copies.append(copy)
 
     shape = (32, 256)
     m2 = lax.broadcasted_iota(jnp.int32, shape, 0)
@@ -296,7 +322,10 @@
 
     for copy in copies:
         copy.wait_recv()
-    surround(range(6), True)
+    rest = jnp.zeros((120, 128), f32)
+    right = jnp.transpose(jnp.concatenate([r["cols_in"][0], rest], axis=0))
+    left = jnp.transpose(jnp.concatenate([rest, r["cols_in"][1]], axis=0))
+    surround(range(6), (right, left))
     for i in (0, 8, 9):
         layer_1(i)
     layer_1_ends(range(1, 8))
@@ -390,15 +419,6 @@
             return 0
 
         lax.fori_loop(0, size - 1, go, 0)
-
-    def x_peer(step):
-        return (a + far_first(step, GX)) % GX
-
-    def y_peer(step):
-        return 2 * ((y_at + far_first(step, 8)) % 8) + x_hi
-
-    def all_y_peer(step):
-        return (b + far_first(step, GY)) % GY
 
     wait_for(rsem.at[0], r1.at[pl.ds(0, GY - 1)])
 
@@ -553,8 +573,10 @@
     }
     scratch |= {
         "rows_in": pltpu.VMEM((2, 2, 8, 256), f32),
-        "cols_in": pltpu.VMEM((2, 2, 32, 128), f32),
-        "corner_in": pltpu.VMEM((2, 2, 2, 8, 128), f32),
+        "cols_in": pltpu.VMEM((2, 8, 128), f32),
+        "corner_in": pltpu.VMEM((2, 2, 8, 128), f32),
+        "cols_out": pltpu.VMEM((2, 8, 128), f32),
+        "corner_out": pltpu.VMEM((2, 2, 8, 128), f32),
         "fs": pltpu.VMEM((6, 2, 3, 56, 128), f32),
         "k1": pltpu.VMEM((48, 256), f32),
         "k2": pltpu.VMEM((3, 256, 384), bf16),
@@ -578,8 +600,8 @@
         "s6": pltpu.VMEM((16, 16, 128), f32),
         "r6": pltpu.VMEM((8, 2, 16, 128), f32),
         "lsem": pltpu.SemaphoreType.DMA((len(inputs),)),
-        "hssem": pltpu.SemaphoreType.DMA((16,)),
-        "hrsem": pltpu.SemaphoreType.DMA((16,)),
+        "hssem": pltpu.SemaphoreType.DMA((10,)),
+        "hrsem": pltpu.SemaphoreType.DMA((10,)),
         "ssem": pltpu.SemaphoreType.DMA((6,)),
         "rsem": pltpu.SemaphoreType.DMA((6,)),
     }

time: 61.5 us -> 60.5 us (0.984)
  Pallas kernels: 58.9 us -> 58.2 us
    pallas_call x1, Pallas kernels: 58.9 us -> 58.2 us  [on_device(): pl.pallas_call(functools.partial(kernel, names), out_shape=jax.ShapeDtype...]
where the time goes in v5:
time: 60.5 us; the launch traced here: 60.3 us
  Pallas kernels  58.2 us (96%)
  local copies, waits for them, and re-layouts  1.4 us (2%)
  between operations  0.64 us (1%)
    pallas_call x1, Pallas kernels, on_device(): pl.pallas_call(functools.partial(kernel, names), out_shape=jax.ShapeDtype...  58.2 us
    squeeze x1, local copies, waits for them, and re-layouts, on_device(): return (result[0], result[1])  1.4 us

profile of v5, /device:TPU:1, one launch (start us, length us, event | category | flops | bytes accessed | tf_op | source)
XLA Modules:
  0.0 60.3 jit_solution(11291822778413676848)
XLA Ops:
  0.6 58.2 %step.1 = f32[2,32,256]{2,1,0:T(8,128)} custom-call(f32[32,256]{1,0:T(8,128)} %refs_0_.1, f32[32,256]{1,0:T(8,128)} %refs_1_.1, bf16[9,2,64]{2,1,0:T(2,128)(2,1)} %bitcast.7, bf16[9,64,64]{2,1,0:T(8,128)(2,1)} %refs_3_.1, bf16[9,16,64]{2,1,0:T(8,128)(2,1)} %refs_4_.1, f32[1,64]{1,0:T(1,128)} %bitcast.8, f32[1,64]{1,0:T(1,128)} %bitcast.9, f32[16]{0:T(128)} %refs_7_.1, ...), custom_call_target="tpu_custom_call" | custom-call | tf_op jit(solution)/shard_map/step/pallas_call | solution.py:609
  58.9 1.4 %slice_bitcast_fusion = (f32[32,256]{1,0:T(8,128)}, f32[32,256]{1,0:T(8,128)}) fusion(f32[2,32,256]{2,1,0:T(8,128)} %step.1), kind=kLoop, calls=%fused_computation | loop fusion | bytes 131072 | tf_op jit(solution)/shard_map/squeeze | solution.py:618

commit v6 on v5

--- a/solution.py
+++ b/solution.py
@@ -51,7 +51,7 @@
     t_a = np.stack([triple_left(real_left(root(np.outer(k, n16), 16)) * sign[None, :]) for k in halves])
     t_a2 = np.stack([triple_left(real_left(root(np.outer(n16, k), 16)) * sign[:, None]) for k in halves])
     mid = root(np.outer(n256, n256), 256)
-    t_b = np.stack(split_bf16(np.block([[mid.real, mid.imag], [-mid.imag, mid.real]])))
+    t_b = np.stack(split_bf16(np.concatenate([mid.real, mid.imag], axis=1)))
     turn = [root(np.outer(k, n256), 4096) for k in halves]
     tw = np.stack([np.stack([w.real, w.imag]) for w in turn]).astype(np.float32)
     t_s = np.stack(
@@ -78,12 +78,15 @@
     return jnp.dot(table, triple(value), preferred_element_type=f32)
 
 
-def right_product(value, t_b):
-    rows = value.shape[0]
+def right_product(re, im, t_b):
+    rows = re.shape[0]
+    value = jnp.concatenate([re, im], axis=0)
     hi = value.astype(bf16)
     lo = (value - hi.astype(f32)).astype(bf16)
     both = jnp.dot(jnp.concatenate([hi, lo], axis=0), t_b[0], preferred_element_type=f32)
-    return both[:rows] + both[rows:] + jnp.dot(hi, t_b[1], preferred_element_type=f32)
+    total = both[: 2 * rows] + both[2 * rows :] + jnp.dot(hi, t_b[1], preferred_element_type=f32)
+    by_re, by_im = total[:, :256], total[:, 256:]
+    return by_re[:rows] - by_im[rows:], by_im[:rows] + by_re[rows:]
 
 
 def nt(left, right):
@@ -110,16 +113,36 @@
     b = lax.axis_index("gy")
     y_at, x_hi = b // 2, b % 2
 
-    def x_peer(step):
-        z = (a % 16 // 2 + far_first(step // 4, 8)) % 8
-        x_lo = (a // 16 + 1 - step % 4 // 2) % 2
-        return x_lo * 16 + z * 2 + (a + 1 - step % 2) % 2
-
-    def y_peer(step):
-        return 2 * ((y_at + far_first(step, 8)) % 8) + x_hi
-
-    def all_y_peer(step):
-        return 2 * ((y_at + far_first(step // 2, 8)) % 8) + (b + 1 - step % 2) % 2
+    z_at, core, x_lo = a % 16 // 2, a % 2, a // 16
+    mates = [(1 - x_lo) * 16 + 1 - core, (1 - x_lo) * 16 + core, x_lo * 16 + 1 - core, x_lo * 16 + core]
+
+    def each_x(go):
+        def some(step, _):
+            z = (z_at + far_first(step, 8)) % 8
+            for end in mates:
+                go(end + 2 * z)
+            return 0
+
+        lax.fori_loop(0, 7, some, 0)
+        for end in mates[:3]:
+            go(end + 2 * z_at)
+
+    def each_y(go):
+        def some(step, _):
+            y = (y_at + far_first(step, 8)) % 8
+            go(2 * y + 1 - x_hi)
+            go(2 * y + x_hi)
+            return 0
+
+        lax.fori_loop(0, 7, some, 0)
+        go(2 * y_at + 1 - x_hi)
+
+    def each_near_y(go):
+        def some(step, _):
+            go(2 * ((y_at + far_first(step, 8)) % 8) + x_hi)
+            return 0
+
+        lax.fori_loop(0, 7, some, 0)
 
     moves = [(-1, -1), (-1, 1), (1, -1), (1, 1), (0, -1), (0, 1), (-1, 0), (1, 0)]
 
@@ -131,16 +154,11 @@
         if dx and dy:
             pl.semaphore_signal(barrier, inc=1, device_id=at(dx, dy), device_id_type=MESH)
 
-    def greet_y(step, _):
-        pl.semaphore_signal(barrier, inc=1, device_id={"gy": all_y_peer(step)}, device_id_type=MESH)
-        return 0
-
-    def greet_x(step, _):
-        pl.semaphore_signal(barrier, inc=1, device_id={"gx": x_peer(step)}, device_id_type=MESH)
-        return 0
-
-    lax.fori_loop(0, GY - 1, greet_y, 0)
-    lax.fori_loop(0, GX - 1, greet_x, 0)
+    def greet(axis):
+        return lambda peer: pl.semaphore_signal(barrier, inc=1, device_id={axis: peer}, device_id_type=MESH)
+
+    each_y(greet("gy"))
+    each_x(greet("gx"))
     local = []
     for n, name in enumerate(("u", "v", "w1", "w2", "w3", "b1", "b2", "b3", "t_a", "t_a2", "t_b", "tw", "t_s", "twr")):
         copy = pltpu.make_async_copy(r[name + "_hbm"], r[name], r["lsem"].at[n])
@@ -410,15 +428,13 @@
     send_block(y_at)
     r1[b] = s1[y_at]
 
-    def send(stage, axis, size, peer_of, src_of, dst):
-        def go(step, _):
-            peer = peer_of(step)
+    def send(stage, axis, each, src_of, dst):
+        def go(peer):
             pltpu.make_async_remote_copy(
                 src_of(peer), dst, ssem.at[stage], rsem.at[stage], device_id={axis: peer}, device_id_type=MESH
             ).start()
-            return 0
-
-        lax.fori_loop(0, size - 1, go, 0)
+
+        each(go)
 
     wait_for(rsem.at[0], r1.at[pl.ds(0, GY - 1)])
 
@@ -431,20 +447,21 @@
         axis=0,
     )
     y = left_product(r["t_a"][x_hi], x)
-    lines = []
+    lines = [[], []]
     for i in range(4):
         yr, yi = y[:8, i * 256 : i * 256 + 256], y[8:, i * 256 : i * 256 + 256]
-        lines.append(jnp.concatenate([yr * tr - yi * ti, yr * ti + yi * tr], axis=1))
-    o = right_product(jnp.concatenate(lines, axis=0), r["t_b"])
+        lines[0].append(yr * tr - yi * ti)
+        lines[1].append(yr * ti + yi * tr)
+    o = right_product(*(jnp.concatenate(line, axis=0) for line in lines), r["t_b"])
     s2, r2 = r["s2"], r["r2"]
     for c in range(2):
         for rp in range(2):
             for h in range(2):
-                cols = slice(c * 256 + h * 128, c * 256 + h * 128 + 128)
-                pair = swap_halves(o[rp * 16 : rp * 16 + 8, cols], o[rp * 16 + 8 : rp * 16 + 16, cols], lane)
+                part = o[c][rp * 16 : rp * 16 + 16, h * 128 : h * 128 + 128]
+                pair = swap_halves(part[:8], part[8:], lane)
                 for low in range(2):
                     s2[:, 2 * h + low, c * 2 + rp, :] = pair[low]
-    send(1, "gx", GX, x_peer, lambda peer: s2.at[peer // 4, peer % 4], r2.at[a])
+    send(1, "gx", each_x, lambda peer: s2.at[peer // 4, peer % 4], r2.at[a])
     r2[a] = s2[a // 4, a % 4]
     wait_for(rsem.at[1], r2.at[pl.ds(0, GX - 1)])
 
@@ -467,7 +484,7 @@
                 pair = swap_halves(value[tp * 16 : tp * 16 + 8], value[tp * 16 + 8 : tp * 16 + 16], lane)
                 for low in range(2):
                     s3[:, c * 8 + (2 * rp + low) * 2 + tp, :] = pair[low]
-    send(2, "gy", 8, y_peer, lambda peer: s3.at[peer // 2], r3.at[y_at])
+    send(2, "gy", each_near_y, lambda peer: s3.at[peer // 2], r3.at[y_at])
     r3[y_at] = s3[y_at]
     wait_for(rsem.at[2], r3.at[pl.ds(0, 7)])
     x = jnp.concatenate(
@@ -491,7 +508,7 @@
             for tp in range(2):
                 row = c * 32 + i * 8
                 s4[:, c * 8 + i * 2 + tp, :] = y[row : row + 8, tp * 128 : tp * 128 + 128]
-    send(3, "gy", 8, y_peer, lambda peer: s4.at[peer // 2], r4.at[y_at])
+    send(3, "gy", each_near_y, lambda peer: s4.at[peer // 2], r4.at[y_at])
     r4[y_at] = s4[y_at]
     wait_for(rsem.at[3], r4.at[pl.ds(0, 7)])
     halves = [[], []]
@@ -512,7 +529,7 @@
     for c in range(2):
         for rp in range(2):
             s5[:, c * 2 + rp, :] = y[c * 32 : c * 32 + 32, rp * 128 : rp * 128 + 128]
-    send(4, "gx", GX, x_peer, lambda peer: s5.at[peer], r5.at[a // 4, a % 4])
+    send(4, "gx", each_x, lambda peer: s5.at[peer], r5.at[a // 4, a % 4])
     r5[a // 4, a % 4] = s5[a]
     wait_for(rsem.at[4], s5.at[pl.ds(0, GX - 1)])
     lines = [[None] * 4 for _ in range(4)]
@@ -522,11 +539,14 @@
                 pair = swap_halves(r5[:, 2 * h, c * 2 + rp, :], r5[:, 2 * h + 1, c * 2 + rp, :], lane)
                 for low in range(2):
                     lines[2 * rp + low][c * 2 + h] = pair[low]
-    x = jnp.concatenate([jnp.concatenate(line, axis=1) for line in lines], axis=0)
-    o = right_product(x, r["t_b"])
+    x = [
+        jnp.concatenate([jnp.concatenate(line[c * 2 : c * 2 + 2], axis=1) for line in lines], axis=0)
+        for c in range(2)
+    ]
+    o = right_product(*x, r["t_b"])
     lines = [[], []]
     for i in range(4):
-        yr, yi = o[i * 8 : i * 8 + 8, :256], o[i * 8 : i * 8 + 8, 256:]
+        yr, yi = o[0][i * 8 : i * 8 + 8], o[1][i * 8 : i * 8 + 8]
         lines[0].append(yr * tr - yi * ti)
         lines[1].append(yr * ti + yi * tr)
     x = jnp.concatenate([jnp.concatenate(line, axis=1) for line in lines], axis=0)
@@ -537,7 +557,7 @@
             for h in range(2):
                 at_lane = i * 256 + h * 128
                 s6[:, c * 8 + h * 4 + i, :] = y[c * 16 : c * 16 + 16, at_lane : at_lane + 128]
-    send(5, "gy", GY, all_y_peer, lambda peer: s6.at[peer], r6.at[y_at, x_hi])
+    send(5, "gy", each_y, lambda peer: s6.at[peer], r6.at[y_at, x_hi])
     r6[y_at, x_hi] = s6[b]
     wait_for(rsem.at[5], s6.at[pl.ds(0, GY - 1)])
     back = r["back"]

time: 60.5 us -> 60 us (level)
  Pallas kernels: 58.2 us -> 57.4 us
    pallas_call x1, Pallas kernels: 58.2 us -> 57.4 us  [on_device(): pl.pallas_call(functools.partial(kernel, names), out_shape=jax.ShapeDtype...]
where the time goes in v6:
time: 60 us; the launch traced here: 59.5 us
  Pallas kernels  57.4 us (96%)
  local copies, waits for them, and re-layouts  1.4 us (2%)
  between operations  0.64 us (1%)
    pallas_call x1, Pallas kernels, on_device(): pl.pallas_call(functools.partial(kernel, names), out_shape=jax.ShapeDtype...  57.4 us
    squeeze x1, local copies, waits for them, and re-layouts, on_device(): return (result[0], result[1])  1.4 us

profile of v6, /device:TPU:1, one launch (start us, length us, event | category | flops | bytes accessed | tf_op | source)
XLA Modules:
  0.0 59.5 jit_solution(14688403735579299251)
XLA Ops:
  0.6 57.4 %step.1 = f32[2,32,256]{2,1,0:T(8,128)} custom-call(f32[32,256]{1,0:T(8,128)} %refs_0_.1, f32[32,256]{1,0:T(8,128)} %refs_1_.1, bf16[9,2,64]{2,1,0:T(2,128)(2,1)} %bitcast.7, bf16[9,64,64]{2,1,0:T(8,128)(2,1)} %refs_3_.1, bf16[9,16,64]{2,1,0:T(8,128)(2,1)} %refs_4_.1, f32[1,64]{1,0:T(1,128)} %bitcast.8, f32[1,64]{1,0:T(1,128)} %bitcast.9, f32[16]{0:T(128)} %refs_7_.1, ...), custom_call_target="tpu_custom_call" | custom-call | tf_op jit(solution)/shard_map/step/pallas_call | solution.py:629
  58.0 1.4 %slice_bitcast_fusion = (f32[32,256]{1,0:T(8,128)}, f32[32,256]{1,0:T(8,128)}) fusion(f32[2,32,256]{2,1,0:T(8,128)} %step.1), kind=kLoop, calls=%fused_computation | loop fusion | bytes 131072 | tf_op jit(solution)/shard_map/squeeze | solution.py:638

commit v7 on v6

--- a/solution.py
+++ b/solution.py
@@ -418,8 +418,8 @@
         y = third(block_of(step + 1))
         i = block_of(step)
         advance(i)
+        send_block(i)
         keep(y)
-        send_block(i)
         return 0
 
     keep(third(block_of(0)))

time: 60 us -> 59.9 us (level)
  no operation moved by 1% of the time
where the time goes in v7:
time: 59.9 us; the launch traced here: 59.7 us
  Pallas kernels  57.6 us (96%)
  local copies, waits for them, and re-layouts  1.4 us (2%)
  between operations  0.64 us (1%)
    pallas_call x1, Pallas kernels, on_device(): pl.pallas_call(functools.partial(kernel, names), out_shape=jax.ShapeDtype...  57.6 us
    squeeze x1, local copies, waits for them, and re-layouts, on_device(): return (result[0], result[1])  1.4 us

profile of v7, /device:TPU:1, one launch (start us, length us, event | category | flops | bytes accessed | tf_op | source)
XLA Modules:
  0.0 59.7 jit_solution(4534108871757213308)
XLA Ops:
  0.6 57.6 %step.1 = f32[2,32,256]{2,1,0:T(8,128)} custom-call(f32[32,256]{1,0:T(8,128)} %refs_0_.1, f32[32,256]{1,0:T(8,128)} %refs_1_.1, bf16[9,2,64]{2,1,0:T(2,128)(2,1)} %bitcast.7, bf16[9,64,64]{2,1,0:T(8,128)(2,1)} %refs_3_.1, bf16[9,16,64]{2,1,0:T(8,128)(2,1)} %refs_4_.1, f32[1,64]{1,0:T(1,128)} %bitcast.8, f32[1,64]{1,0:T(1,128)} %bitcast.9, f32[16]{0:T(128)} %refs_7_.1, ...), custom_call_target="tpu_custom_call" | custom-call | tf_op jit(solution)/shard_map/step/pallas_call | solution.py:629
  58.3 1.4 %slice_bitcast_fusion = (f32[32,256]{1,0:T(8,128)}, f32[32,256]{1,0:T(8,128)}) fusion(f32[2,32,256]{2,1,0:T(8,128)} %step.1), kind=kLoop, calls=%fused_computation | loop fusion | bytes 131072 | tf_op jit(solution)/shard_map/squeeze | solution.py:638
